TPU v7x, 32 devices: a whole 2x2x4 slice. The times are simulated.
32 devices in a mesh: freq: 4 (over y, x), tile: 8 (over z, core).
Axes of the slice: x: 2, y: 2, z: 4, core: 2. Of those that a mesh axis runs over, the one named last changes fastest.
Arguments:
- x_field: bfloat16 [4, 2, 5120, 256], P('freq', None, 'tile'), may hold values from -6 to 6
- data: bfloat16 [4, 2, 5120, 256], P('freq', None, 'tile'), may hold values from -6 to 6
- u_bases: bfloat16 [4, 8, 8, 128, 2, 640], P('freq', 'tile'), may hold values from -0.21875 to 0.21875
- v_bases: bfloat16 [4, 8, 8, 128, 2, 640], P('freq', None, 'tile'), may hold values from -0.15625 to 0.15625
- ranks: int32 [4, 8, 8], P('freq'), may hold values from 49 to 96, as said below
- onset: int32 [5120, 256], P(('tile', 'freq')), may hold values from 0 to 3
Outputs:
- gradient: float32 [8, 5120, 256], P(None, ('tile', 'freq'))
Inputs may be any that keep to these rules, and one draw needn't show every extreme that they name: ranks[f,r,c] is the rank of tile (r, c) at frequency f; it is at most 96, and equal to 96 for some tile of every frequency.
All inputs are finite; a program needn't handle non-finite values.
Results may differ from a plain program's by a relative error of at most 0.0055.
Values may be sent and summed in bfloat16 or wider, within the bound.
No kernel may reach another device: no remote copies, remote signals or barrier semaphores. Data moves between devices by JAX's collectives and lax.ppermute only.
A program may use at most 64 MiB of HBM per device.

v0:
```python
import functools
import math

import jax
import jax.numpy as jnp
from jax import lax
from jax.experimental import pallas as pl
from jax.experimental.pallas import tpu as pltpu
from jax.sharding import PartitionSpec as P


RMAX = 96
LANES = 128
BF16 = jnp.bfloat16
F32 = jnp.float32
VMEM = pl.BlockSpec(memory_space=pltpu.VMEM)
SMEM = pl.BlockSpec(memory_space=pltpu.SMEM)
ANY = pl.BlockSpec(memory_space=pl.ANY)
HBM = pl.BlockSpec(memory_space=pltpu.MemorySpace.HBM)


def params():
    return pltpu.CompilerParams(vmem_limit_bytes=48 * 1024 * 1024)


def masked(value, rank):
    level = lax.broadcasted_iota(jnp.int32, value.shape, 0)
    return jnp.where(level < rank, value, 0.0).astype(BF16)


def cost(flops):
    return pl.CostEstimate(flops=flops, bytes_accessed=10**7, transcendentals=0)


def coeff_kernel(ks, group, *refs):
    rank_hbm, v_hbm, x_hbm, _ = refs[:4]
    outs = refs[4 : 4 + len(ks)]
    rank_ref, factors, field, wide, product, sems, field_sem, rank_sem = refs[4 + len(ks) :]
    me = lax.axis_index("tile")
    stations = field.shape[1]
    virtual = field.shape[2]
    rank_copy = pltpu.make_async_copy(rank_hbm, rank_ref, rank_sem)
    field_copy = pltpu.make_async_copy(x_hbm, field, field_sem)
    copies = [
        pltpu.make_async_copy(v_hbm.at[me ^ k, pl.ds(0, RMAX)], factors.at[i], sems.at[i])
        for i, k in enumerate(ks)
    ]
    field_copy.start()
    for copy in copies:
        copy.start()
    rank_copy.start()
    field_copy.wait()
    wide[:, :virtual] = field[0]
    wide[:, virtual:] = field[1]
    rank_copy.wait()
    parts = 2 * virtual // LANES
    half = parts // 2
    for start in range(0, len(ks), group):
        for i in range(start, start + group):
            copies[i].wait()
        left = factors[pl.ds(start, group)].reshape(group * 2 * RMAX, stations)
        result = jnp.dot(left, wide[...], preferred_element_type=F32)
        for j in range(parts):
            product[j] = result[:, j * LANES : (j + 1) * LANES]
        for i in range(group):
            out = outs[start + i]
            rank = rank_ref[me ^ ks[start + i], me]
            base = i * 2 * RMAX
            even = [product[j, pl.ds(base, RMAX, stride=2), :] for j in range(parts)]
            odd = [product[j, pl.ds(base + 1, RMAX, stride=2), :] for j in range(parts)]
            for j in range(half):
                real = masked(even[j] + odd[half + j], rank)
                imag = masked(even[half + j] - odd[j], rank)
                out[:, j * LANES : (j + 1) * LANES] = real
                out[:, (half + j) * LANES : (half + j + 1) * LANES] = imag


def coeff_blocks(ranks, v, x, after, ks, group):
    stations, virtual = x.shape[1], x.shape[2]
    return pl.pallas_call(
        functools.partial(coeff_kernel, ks, group),
        out_shape=[jax.ShapeDtypeStruct((RMAX, 2 * virtual), BF16) for _ in ks],
        in_specs=[HBM, HBM, HBM, ANY],
        out_specs=[VMEM for _ in ks],
        scratch_shapes=[
            pltpu.SMEM(ranks.shape, jnp.int32),
            pltpu.VMEM((len(ks), RMAX, 2, stations), BF16),
            pltpu.VMEM((2, stations, virtual), BF16),
            pltpu.VMEM((stations, 2 * virtual), BF16),
            pltpu.VMEM((2 * virtual // LANES, group * 2 * RMAX, LANES), F32),
            pltpu.SemaphoreType.DMA((len(ks),)),
            pltpu.SemaphoreType.DMA,
            pltpu.SemaphoreType.DMA,
        ],
        compiler_params=params(),
        cost_estimate=cost(10**9),
        name="coeff_blocks",
    )(ranks, v, x, after)


def prepare_kernel(want_rows, *refs):
    w_hbm, _ = refs[:2]
    turned_ref = refs[2]
    if want_rows:
        rows_ref = refs[3]
        factors, spread, paired, sems = refs[4:]
    else:
        rows_ref = None
        factors, spread, paired, sems = refs[3:]
    count = factors.shape[0]
    stations = factors.shape[3]
    columns = stations // LANES
    copies = [
        pltpu.make_async_copy(w_hbm.at[r, pl.ds(0, RMAX)], factors.at[r], sems.at[r])
        for r in range(count)
    ]
    for copy in copies:
        copy.start()
    for r in range(count):
        copies[r].wait()
        flat = factors[r].reshape(2 * RMAX, stations).astype(F32)
        for j in range(columns):
            spread[j] = flat[:, j * LANES : (j + 1) * LANES]
        for p in range(2):
            for j in range(columns):
                piece = spread[j, pl.ds(p, RMAX, stride=2), :].astype(BF16)
                row = (2 * p + r % 2) * RMAX
                paired[row : row + RMAX, j * LANES : (j + 1) * LANES] = piece
                if rows_ref is not None:
                    column = p * stations + j * LANES
                    rows_ref[r * RMAX : (r + 1) * RMAX, column : column + LANES] = piece
        if r % 2:
            for i in range(4 * RMAX // LANES):
                block = paired[i * LANES : (i + 1) * LANES, :]
                turned_ref[r // 2, :, i * LANES : (i + 1) * LANES] = block.T


def prepare(w, after, want_rows):
    count, _, _, stations = w.shape
    outs = [jax.ShapeDtypeStruct((count // 2, stations, 4 * RMAX), BF16)]
    if want_rows:
        outs.append(jax.ShapeDtypeStruct((count * RMAX, 2 * stations), BF16))
    return pl.pallas_call(
        functools.partial(prepare_kernel, want_rows),
        out_shape=outs,
        in_specs=[HBM, ANY],
        out_specs=[VMEM for _ in outs],
        scratch_shapes=[
            pltpu.VMEM((count, RMAX, 2, stations), BF16),
            pltpu.VMEM((stations // LANES, 2 * RMAX, LANES), F32),
            pltpu.VMEM((4 * RMAX, stations), BF16),
            pltpu.SemaphoreType.DMA((count,)),
        ],
        compiler_params=params(),
        cost_estimate=cost(10**9),
        name="prepare",
    )(w, after)


def apply_pairs(bases, blocks, turned_ref, stack):
    me = lax.axis_index("tile")
    virtual = blocks[0].shape[1] // 2
    total = None
    for i, base in enumerate(bases):
        for b in range(2):
            block = blocks[2 * i + b]
            slot = (me ^ b) & 1
            rows = pl.ds(pl.multiple_of(slot * RMAX, RMAX), RMAX)
            stack[i, rows, :] = block[...]
            rows = pl.ds(pl.multiple_of((slot + 2) * RMAX, RMAX), RMAX)
            stack[i, rows, :virtual] = -block[:, virtual:]
            stack[i, rows, virtual:] = block[:, :virtual]
        term = jnp.dot(
            turned_ref[(me ^ base) >> 1], stack[i], preferred_element_type=F32
        )
        total = term if total is None else total + term
    return total


def partial_kernel(bases, *refs):
    turned_ref = refs[0]
    blocks = refs[1 : 1 + 2 * len(bases)]
    out_ref, stack = refs[1 + 2 * len(bases) :]
    out_ref[...] = apply_pairs(bases, blocks, turned_ref, stack)


def partial_sum(turned, bases, blocks):
    stations = turned.shape[1]
    width = blocks[0].shape[1]
    return pl.pallas_call(
        functools.partial(partial_kernel, bases),
        out_shape=jax.ShapeDtypeStruct((stations, width), F32),
        in_specs=[VMEM] * (1 + len(blocks)),
        out_specs=VMEM,
        scratch_shapes=[pltpu.VMEM((len(bases), 4 * RMAX, width), BF16)],
        compiler_params=params(),
        cost_estimate=cost(10**9),
        name="partial_sum",
    )(turned, *blocks)


def adjoint_outputs(ks, rank_ref, rows_ref, stacked, result, outs):
    me = lax.axis_index("tile")
    for i in range(0, len(ks), 2):
        pair = (me ^ ks[i]) >> 1
        rows = pl.ds(pl.multiple_of(pair * 2 * RMAX, 2 * RMAX), 2 * RMAX)
        product = jnp.dot(rows_ref[rows, :], stacked[...], preferred_element_type=F32)
        for b in range(2):
            result[b * RMAX : (b + 1) * RMAX, :] = masked(
                product[b * RMAX : (b + 1) * RMAX, :], rank_ref[me, 2 * pair + b]
            )
        for b in range(2):
            slot = (me ^ ks[i + b]) & 1
            outs[i + b][...] = result[pl.ds(pl.multiple_of(slot * RMAX, RMAX), RMAX), :]


def residual_kernel(base, ks, *refs):
    rank_ref, rows_ref, turned_ref, data_ref, partial_ref = refs[:5]
    blocks = refs[5:7]
    outs = refs[7 : 7 + len(ks)]
    stacked, stack, result = refs[7 + len(ks) :]
    stations, virtual = data_ref.shape[1], data_ref.shape[2]
    predicted = partial_ref[...] + apply_pairs((base,), blocks, turned_ref, stack)
    real = (predicted[:, :virtual] - data_ref[0].astype(F32)).astype(BF16)
    imag = (predicted[:, virtual:] - data_ref[1].astype(F32)).astype(BF16)
    stacked[:stations, :virtual] = real
    stacked[:stations, virtual:] = imag
    stacked[stations:, :virtual] = imag
    stacked[stations:, virtual:] = -real
    adjoint_outputs(ks, rank_ref, rows_ref, stacked, result, outs)


def residual_blocks(ranks, rows, turned, data, partial, base, blocks, ks):
    stations, virtual = data.shape[1], data.shape[2]
    outs = [jax.ShapeDtypeStruct((RMAX, 2 * virtual), BF16) for _ in ks]
    outs.append(jax.ShapeDtypeStruct((2 * stations, 2 * virtual), BF16))
    return pl.pallas_call(
        functools.partial(residual_kernel, base, ks),
        out_shape=outs,
        in_specs=[SMEM] + [VMEM] * 6,
        out_specs=[VMEM for _ in outs],
        scratch_shapes=[
            pltpu.VMEM((1, 4 * RMAX, 2 * virtual), BF16),
            pltpu.VMEM((2 * RMAX, 2 * virtual), BF16),
        ],
        compiler_params=params(),
        cost_estimate=cost(10**9),
        name="residual_blocks",
    )(ranks, rows, turned, data, partial, *blocks)


def adjoint_kernel(ks, *refs):
    rank_ref, rows_ref, stacked = refs[:3]
    outs = refs[3 : 3 + len(ks)]
    (result,) = refs[3 + len(ks) :]
    adjoint_outputs(ks, rank_ref, rows_ref, stacked, result, outs)


def adjoint_blocks(ranks, rows, stacked, ks):
    width = stacked.shape[1]
    return pl.pallas_call(
        functools.partial(adjoint_kernel, ks),
        out_shape=[jax.ShapeDtypeStruct((RMAX, width), BF16) for _ in ks],
        in_specs=[SMEM, VMEM, VMEM],
        out_specs=[VMEM for _ in ks],
        scratch_shapes=[pltpu.VMEM((2 * RMAX, width), BF16)],
        compiler_params=params(),
        cost_estimate=cost(10**9),
        name="adjoint_blocks",
    )(ranks, rows, stacked)


def spectrum_kernel(base, freqs, *refs):
    turned_ref, partial_ref = refs[:2]
    blocks = refs[2:4]
    outs = refs[4 : 4 + freqs]
    stack, spectrum = refs[4 + freqs :]
    mine = lax.axis_index("freq")
    spectrum[...] = partial_ref[...] + apply_pairs((base,), blocks, turned_ref, stack)
    share = outs[0].shape[0]
    for k in range(freqs):
        rows = pl.ds(pl.multiple_of((mine ^ k) * share, 8), share)
        outs[k][...] = spectrum[rows, :].astype(BF16)


def spectrum_blocks(turned, partial, base, blocks, freqs):
    stations, width = partial.shape
    return pl.pallas_call(
        functools.partial(spectrum_kernel, base, freqs),
        out_shape=[jax.ShapeDtypeStruct((stations // freqs, width), BF16) for _ in range(freqs)],
        in_specs=[VMEM] * 4,
        out_specs=[VMEM] * freqs,
        scratch_shapes=[
            pltpu.VMEM((1, 4 * RMAX, width), BF16),
            pltpu.VMEM((stations, width), F32),
        ],
        compiler_params=params(),
        cost_estimate=cost(10**9),
        name="spectrum_blocks",
    )(turned, partial, *blocks)


def traces_kernel(freqs, *refs):
    onset_ref = refs[0]
    blocks = refs[1 : 1 + freqs]
    out_ref, gathered = refs[1 + freqs :]
    mine = lax.axis_index("freq")
    virtual = onset_ref.shape[1]
    for k in range(freqs):
        gathered[mine ^ k] = blocks[k][...]
    times = 2 * freqs
    scaling = 1.0 / math.sqrt(freqs)
    onset = onset_ref[...]
    for t in range(freqs):
        sums = [None, None]
        for f in range(freqs):
            turn = (f + 1) * t % times
            angle = 2.0 * math.pi * turn / times
            quarter = 4 * turn % times == 0
            terms = []
            for part, weight in ((0, math.cos(angle)), (1, -math.sin(angle))):
                if quarter:
                    weight = float(round(weight))
                if weight != 0.0:
                    value = gathered[f, :, part * virtual : (part + 1) * virtual]
                    terms.append(value.astype(F32) * (weight * scaling))
            for term in terms:
                old = sums[f % 2]
                sums[f % 2] = term if old is None else old + term
        odd, even = sums
        out_ref[t] = jnp.where(t >= onset, even + odd, 0.0)
        out_ref[t + freqs] = jnp.where(t + freqs >= onset, even - odd, 0.0)


def gated_traces(onset, blocks):
    freqs = len(blocks)
    share, virtual = onset.shape
    return pl.pallas_call(
        functools.partial(traces_kernel, freqs),
        out_shape=jax.ShapeDtypeStruct((2 * freqs, share, virtual), F32),
        in_specs=[VMEM] * (1 + freqs),
        out_specs=VMEM,
        scratch_shapes=[pltpu.VMEM((freqs, share, 2 * virtual), BF16)],
        compiler_params=params(),
        name="gated_traces",
    )(onset, *blocks)


def send(block, axis, k):
    count = lax.axis_size(axis)
    return lax.ppermute(block, axis, [(i, i ^ k) for i in range(count)])


def exchange(ks, blocks):
    return {k: send(b, "tile", k) if k else b for k, b in zip(ks, blocks)}


def pick(arrived, bases):
    return [arrived[base + b] for base in bases for b in range(2)]


def pair_bases(count):
    return list(range(count - 2, -1, -2))


def peer_order(count):
    bases = pair_bases(count)
    half = len(bases) // 2
    far = tuple(base + b for base in bases[:half] for b in range(2))
    near = tuple(base + b for base in bases[half:] for b in range(2))
    return far, near


def hbm(array):
    return pltpu.with_memory_space_constraint(array, pltpu.MemorySpace.HBM)


def body(x_field, data, u_bases, v_bases, ranks, onset):
    count = lax.axis_size("tile")
    freqs = lax.axis_size("freq")
    table = ranks[0]
    u = hbm(u_bases[0, 0])
    v = hbm(v_bases[0, :, 0])
    x = hbm(x_field[0])
    late = count // 2
    early = tuple(base for base in pair_bases(count) if base != late)
    far, near = peer_order(count)
    blocks = coeff_blocks(hbm(table), v, x, table, far, 2)
    arrived = exchange(far, blocks)
    blocks = coeff_blocks(hbm(table), v, x, blocks[0], near, 2)
    arrived |= exchange(near, blocks)
    u_turned, u_rows = prepare(u, blocks[0], True)
    partial = partial_sum(u_turned, early, pick(arrived, early))
    *blocks, stacked = residual_blocks(
        table, u_rows, u_turned, data[0], partial, late, pick(arrived, (late,)), far
    )
    returned = exchange(far, blocks)
    blocks = adjoint_blocks(table, u_rows, stacked, near)
    returned |= exchange(near, blocks)
    (v_turned,) = prepare(v, stacked, False)
    partial = partial_sum(v_turned, early, pick(returned, early))
    spectrum = spectrum_blocks(v_turned, partial, late, pick(returned, (late,)), freqs)
    spectra = [send(block, "freq", k) if k else block for k, block in enumerate(spectrum)]
    return gated_traces(onset, spectra)


def solution(mesh):
    in_specs = (
        P("freq", None, "tile", None),
        P("freq", None, "tile", None),
        P("freq", "tile", None, None, None, None),
        P("freq", None, "tile", None, None, None),
        P("freq", None, None),
        P(("tile", "freq"), None),
    )
    out_specs = P(None, ("tile", "freq"), None)

    return jax.shard_map(
        body, mesh=mesh, in_specs=in_specs, out_specs=out_specs, check_vma=False
    )
```

profile of v0, /device:TPU:0, one launch (start us, length us, event | category | flops | bytes accessed | tf_op | source)
XLA Modules:
  0.0 60.1 jit_solution(5217434030549303218)
XLA Ops:
  0.0 2.4 %coeff_blocks.2 = (bf16[96,512]{1,0:T(8,128)(2,1)S(1)}, bf16[96,512]{1,0:T(8,128)(2,1)S(1)}, bf16[96,512]{1,0:T(8,128)(2,1)S(1)}, bf16[96,512]{1,0:T(8,128)(2,1)S(1)}) custom-call(s32[8,8]{1,0:T(8,128)} %bitcast.6, bf16[8,128,2,640]{3,2,1,0:T(2,128)(2,1)} %bitcast.11, bf16[2,640,256]{2,1,0:T(8,128)(2,1)} %bitcast.15, s32[8,8]{1,0:T(8,128)} %bitcast.7), custom_call_target="tpu_custom_call" | custom-call | flops 1000000000 | bytes 10000000 | tf_op jit(solution)/shard_map/coeff_blocks/pallas_call | solution.py:80
  2.4 4.6 %collective-permute-start.1 = (bf16[96,512]{1,0:T(8,128)(2,1)S(1)}, bf16[96,512]{1,0:T(8,128)(2,1)S(1)}, u32[]{:S(2)}, u32[]{:S(2)}) collective-permute-start(bf16[96,512]{1,0:T(8,128)(2,1)S(1)} %get-tuple-element.32), channel_id=1, source_target_pairs={{0,7},{1,6},{2,5},{3,4},{4,3},{5,2},{6,1},{7,0},{8,15},{9,14},{10,... | collective-permute-start | bytes 294920 | tf_op jit(solution)/shard_map/ppermute | solution.py:351
  7.0 0.6 %collective-permute-start = (bf16[96,512]{1,0:T(8,128)(2,1)S(1)}, bf16[96,512]{1,0:T(8,128)(2,1)S(1)}, u32[]{:S(2)}, u32[]{:S(2)}) collective-permute-start(bf16[96,512]{1,0:T(8,128)(2,1)S(1)} %get-tuple-element.28.refs_3_), channel_id=1, source_target_pairs={{0,6},{1,7},{2,4},{3,5},{4,2},{5,3},{6,0},{7,1},{8,14},{9,15},{10,... | collective-permute-start | bytes 294920 | tf_op jit(solution)/shard_map/ppermute | solution.py:351
  7.6 2.4 %coeff_blocks.3 = (bf16[96,512]{1,0:T(8,128)(2,1)S(1)}, bf16[96,512]{1,0:T(8,128)(2,1)S(1)}, bf16[96,512]{1,0:T(8,128)(2,1)S(1)}, bf16[96,512]{1,0:T(8,128)(2,1)S(1)}) custom-call(s32[8,8]{1,0:T(8,128)} %bitcast.8, bf16[8,128,2,640]{3,2,1,0:T(2,128)(2,1)} %bitcast.12, bf16[2,640,256]{2,1,0:T(8,128)(2,1)} %bitcast.16, ...), custom_call_target="tpu_custom_call" | custom-call | flops 1000000000 | bytes 10000000 | tf_op jit(solution)/shard_map/coeff_blocks/pallas_call | solution.py:80
  10.0 0.1 collective-permute-start.4
  10.1 2.0 %collective-permute-start.2 = (bf16[96,512]{1,0:T(8,128)(2,1)S(1)}, bf16[96,512]{1,0:T(8,128)(2,1)S(1)}, u32[]{:S(2)}, u32[]{:S(2)}) collective-permute-start(bf16[96,512]{1,0:T(8,128)(2,1)S(1)} %get-tuple-element.29.refs_1_), channel_id=1, source_target_pairs={{0,2},{1,3},{2,0},{3,1},{4,6},{5,7},{6,4},{7,5},{8,10},{9,11},{10,... | collective-permute-start | bytes 294920 | tf_op jit(solution)/shard_map/ppermute | solution.py:351
  12.2 3.6 %collective-permute-start.5 = (bf16[96,512]{1,0:T(8,128)(2,1)S(1)}, bf16[96,512]{1,0:T(8,128)(2,1)S(1)}, u32[]{:S(2)}, u32[]{:S(2)}) collective-permute-start(bf16[96,512]{1,0:T(8,128)(2,1)S(1)} %get-tuple-element.36), channel_id=1, source_target_pairs={{0,4},{1,5},{2,6},{3,7},{4,0},{5,1},{6,2},{7,3},{8,12},{9,13},{10,... | collective-permute-start | bytes 294920 | tf_op jit(solution)/shard_map/ppermute | solution.py:351
  15.8 1.8 %collective-permute-start.6 = (bf16[96,512]{1,0:T(8,128)(2,1)S(1)}, bf16[96,512]{1,0:T(8,128)(2,1)S(1)}, u32[]{:S(2)}, u32[]{:S(2)}) collective-permute-start(bf16[96,512]{1,0:T(8,128)(2,1)S(1)} %get-tuple-element.37), channel_id=1, source_target_pairs={{0,5},{1,4},{2,7},{3,6},{4,1},{5,0},{6,3},{7,2},{8,13},{9,12},{10,... | collective-permute-start | bytes 294920 | tf_op jit(solution)/shard_map/ppermute | solution.py:351
  17.6 3.5 %prepare.2 = (bf16[4,640,384]{2,1,0:T(8,128)(2,1)S(1)}, bf16[768,1280]{1,0:T(8,128)(2,1)S(1)}) custom-call(bf16[8,128,2,640]{3,2,1,0:T(2,128)(2,1)} %bitcast.14, bf16[96,512]{1,0:T(8,128)(2,1)S(1)} %get-tuple-element.29.refs_1_), custom_call_target="tpu_custom_call" | custom-call | flops 1000000000 | bytes 10000000 | tf_op jit(solution)/shard_map/prepare/pallas_call | solution.py:143
  21.2 1.2 %partial_sum.2.refs_4_ = f32[640,512]{1,0:T(8,128)S(1)} custom-call(bf16[4,640,384]{2,1,0:T(8,128)(2,1)S(1)} %get-tuple-element.31.refs_0_.refs_2_, bf16[96,512]{1,0:T(8,128)(2,1)S(1)} %collective-permute-done.refs_1_, bf16[96,512]{1,0:T(8,128)(2,1)S(1)} %collective-permute-done.1.refs_2_, bf16[96,512]{1,0:T(8,128)(2,1)S(1)} %collective-permute-done.2.refs_3_, ...), custom_call_target="tpu_custom_call" | custom-call | flops 1000000000 | bytes 10000000 | tf_op jit(solution)/shard_map/partial_sum/pallas_call | solution.py:190
  22.4 0.9 %collective-permute-done.5.refs_5_ = bf16[96,512]{1,0:T(8,128)(2,1)S(1)} collective-permute-done((bf16[96,512]{1,0:T(8,128)(2,1)S(1)}, bf16[96,512]{1,0:T(8,128)(2,1)S(1)}, u32[]{:S(2)}, u32[]{:S(2)}) %collective-permute-start.5) | collective-permute-done | bytes 98336 | tf_op jit(solution)/shard_map/ppermute | solution.py:351
  23.3 1.8 %collective-permute-done.6.refs_6_ = bf16[96,512]{1,0:T(8,128)(2,1)S(1)} collective-permute-done((bf16[96,512]{1,0:T(8,128)(2,1)S(1)}, bf16[96,512]{1,0:T(8,128)(2,1)S(1)}, u32[]{:S(2)}, u32[]{:S(2)}) %collective-permute-start.6) | collective-permute-done | bytes 98336 | tf_op jit(solution)/shard_map/ppermute | solution.py:351
  25.1 2.8 %residual_blocks.1 = (bf16[96,512]{1,0:T(8,128)(2,1)S(1)}, bf16[96,512]{1,0:T(8,128)(2,1)S(1)}, bf16[96,512]{1,0:T(8,128)(2,1)S(1)}, bf16[96,512]{1,0:T(8,128)(2,1)S(1)}, bf16[1280,512]{1,0:T(8,128)(2,1)S(1)}) custom-call(s32[8,8]{1,0:T(8,128)S(1)} %bitcast.9, bf16[768,1280]{1,0:T(8,128)(2,1)S(1)} %get-tuple-element.30.refs_1_, ...), custom_call_target="tpu_custom_call" | custom-call | flops 1000000000 | bytes 10000000 | tf_op jit(solution)/shard_map/residual_blocks/pallas_call | solution.py:237
  27.9 1.8 %collective-permute-start.7 = (bf16[96,512]{1,0:T(8,128)(2,1)S(1)}, bf16[96,512]{1,0:T(8,128)(2,1)S(1)}, u32[]{:S(2)}, u32[]{:S(2)}) collective-permute-start(bf16[96,512]{1,0:T(8,128)(2,1)S(1)} %get-tuple-element.39), channel_id=1, source_target_pairs={{0,6},{1,7},{2,4},{3,5},{4,2},{5,3},{6,0},{7,1},{8,14},{9,15},{10,... | collective-permute-start | bytes 294920 | tf_op jit(solution)/shard_map/ppermute | solution.py:351
  29.7 1.5 %collective-permute-start.8 = (bf16[96,512]{1,0:T(8,128)(2,1)S(1)}, bf16[96,512]{1,0:T(8,128)(2,1)S(1)}, u32[]{:S(2)}, u32[]{:S(2)}) collective-permute-start(bf16[96,512]{1,0:T(8,128)(2,1)S(1)} %get-tuple-element.40), channel_id=1, source_target_pairs={{0,7},{1,6},{2,5},{3,4},{4,3},{5,2},{6,1},{7,0},{8,15},{9,14},{10,... | collective-permute-start | bytes 294920 | tf_op jit(solution)/shard_map/ppermute | solution.py:351
  31.2 1.3 %adjoint_blocks.1 = (bf16[96,512]{1,0:T(8,128)(2,1)S(1)}, bf16[96,512]{1,0:T(8,128)(2,1)S(1)}, bf16[96,512]{1,0:T(8,128)(2,1)S(1)}, bf16[96,512]{1,0:T(8,128)(2,1)S(1)}) custom-call(s32[8,8]{1,0:T(8,128)S(1)} %bitcast.10, bf16[768,1280]{1,0:T(8,128)(2,1)S(1)} %get-tuple-element.30.refs_1_, bf16[1280,512]{1,0:T(8,128)(2,1)S(1)} %get-tuple-element.38.refs_1_.refs_2_), custom_call_target="tpu_custom_call" | custom-call | flops 1000000000 | bytes 10000000 | tf_op jit(solution)/shard_map/adjoint_blocks/pallas_call | solution.py:261
  32.6 2.0 %collective-permute-start.10 = (bf16[96,512]{1,0:T(8,128)(2,1)S(1)}, bf16[96,512]{1,0:T(8,128)(2,1)S(1)}, u32[]{:S(2)}, u32[]{:S(2)}) collective-permute-start(bf16[96,512]{1,0:T(8,128)(2,1)S(1)} %get-tuple-element.42), channel_id=1, source_target_pairs={{0,3},{1,2},{2,1},{3,0},{4,7},{5,6},{6,5},{7,4},{8,11},{9,10},{10,... | collective-permute-start | bytes 294920 | tf_op jit(solution)/shard_map/ppermute | solution.py:351
  34.6 0.1 collective-permute-start.11
  34.7 0.6 %collective-permute-start.12 = (bf16[96,512]{1,0:T(8,128)(2,1)S(1)}, bf16[96,512]{1,0:T(8,128)(2,1)S(1)}, u32[]{:S(2)}, u32[]{:S(2)}) collective-permute-start(bf16[96,512]{1,0:T(8,128)(2,1)S(1)} %get-tuple-element.45), channel_id=1, source_target_pairs={{0,4},{1,5},{2,6},{3,7},{4,0},{5,1},{6,2},{7,3},{8,12},{9,13},{10,... | collective-permute-start | bytes 294920 | tf_op jit(solution)/shard_map/ppermute | solution.py:351
  35.4 1.2 %collective-permute-done.8.refs_2_ = bf16[96,512]{1,0:T(8,128)(2,1)S(1)} collective-permute-done((bf16[96,512]{1,0:T(8,128)(2,1)S(1)}, bf16[96,512]{1,0:T(8,128)(2,1)S(1)}, u32[]{:S(2)}, u32[]{:S(2)}) %collective-permute-start.8) | collective-permute-done | bytes 98336 | tf_op jit(solution)/shard_map/ppermute | solution.py:351
  36.6 1.7 %collective-permute-start.13 = (bf16[96,512]{1,0:T(8,128)(2,1)S(1)}, bf16[96,512]{1,0:T(8,128)(2,1)S(1)}, u32[]{:S(2)}, u32[]{:S(2)}) collective-permute-start(bf16[96,512]{1,0:T(8,128)(2,1)S(1)} %get-tuple-element.46), channel_id=1, source_target_pairs={{0,5},{1,4},{2,7},{3,6},{4,1},{5,0},{6,3},{7,2},{8,13},{9,12},{10,... | collective-permute-start | bytes 294920 | tf_op jit(solution)/shard_map/ppermute | solution.py:351
  38.3 3.3 %prepare.3.refs_0_ = bf16[4,640,384]{2,1,0:T(8,128)(2,1)S(1)} custom-call(bf16[8,128,2,640]{3,2,1,0:T(2,128)(2,1)} %bitcast.13, bf16[1280,512]{1,0:T(8,128)(2,1)S(1)} %get-tuple-element.38.refs_1_.refs_2_), custom_call_target="tpu_custom_call" | custom-call | flops 1000000000 | bytes 10000000 | tf_op jit(solution)/shard_map/prepare/pallas_call | solution.py:143
  41.6 1.6 %collective-permute-done.10.refs_4_ = bf16[96,512]{1,0:T(8,128)(2,1)S(1)} collective-permute-done((bf16[96,512]{1,0:T(8,128)(2,1)S(1)}, bf16[96,512]{1,0:T(8,128)(2,1)S(1)}, u32[]{:S(2)}, u32[]{:S(2)}) %collective-permute-start.10) | collective-permute-done | bytes 98336 | tf_op jit(solution)/shard_map/ppermute | solution.py:351
  43.3 1.2 %partial_sum.3.refs_1_ = f32[640,512]{1,0:T(8,128)S(1)} custom-call(bf16[4,640,384]{2,1,0:T(8,128)(2,1)S(1)} %prepare.3.refs_0_, bf16[96,512]{1,0:T(8,128)(2,1)S(1)} %collective-permute-done.7.refs_1_, bf16[96,512]{1,0:T(8,128)(2,1)S(1)} %collective-permute-done.8.refs_2_, bf16[96,512]{1,0:T(8,128)(2,1)S(1)} %collective-permute-done.9.refs_3_, ...), custom_call_target="tpu_custom_call" | custom-call | flops 1000000000 | bytes 10000000 | tf_op jit(solution)/shard_map/partial_sum/pallas_call | solution.py:190
  44.5 2.3 %collective-permute-done.13.refs_3_ = bf16[96,512]{1,0:T(8,128)(2,1)S(1)} collective-permute-done((bf16[96,512]{1,0:T(8,128)(2,1)S(1)}, bf16[96,512]{1,0:T(8,128)(2,1)S(1)}, u32[]{:S(2)}, u32[]{:S(2)}) %collective-permute-start.13) | collective-permute-done | bytes 98336 | tf_op jit(solution)/shard_map/ppermute | solution.py:351
  46.8 0.6 %spectrum_blocks.1 = (bf16[160,512]{1,0:T(8,128)(2,1)S(1)}, bf16[160,512]{1,0:T(8,128)(2,1)S(1)}, bf16[160,512]{1,0:T(8,128)(2,1)S(1)}, bf16[160,512]{1,0:T(8,128)(2,1)S(1)}) custom-call(bf16[4,640,384]{2,1,0:T(8,128)(2,1)S(1)} %prepare.3.refs_0_, f32[640,512]{1,0:T(8,128)S(1)} %partial_sum.3.refs_1_, bf16[96,512]{1,0:T(8,128)(2,1)S(1)} %collective-permute-done.12.refs_2_, ...), custom_call_target="tpu_custom_call" | custom-call | flops 1000000000 | bytes 10000000 | tf_op jit(solution)/shard_map/spectrum_blocks/pallas_call | solution.py:288
  47.4 1.6 %collective-permute-start.14 = (bf16[160,512]{1,0:T(8,128)(2,1)S(1)}, bf16[160,512]{1,0:T(8,128)(2,1)S(1)}, u32[]{:S(2)}, u32[]{:S(2)}) collective-permute-start(bf16[160,512]{1,0:T(8,128)(2,1)S(1)} %get-tuple-element.48), channel_id=1, source_target_pairs={{0,8},{8,0},{16,24},{24,16},{1,9},{9,1},{17,25},{25,17},{2,10},{10... | collective-permute-start | bytes 491528 | tf_op jit(solution)/shard_map/ppermute | solution.py:351
  49.0 1.5 %collective-permute-start.15 = (bf16[160,512]{1,0:T(8,128)(2,1)S(1)}, bf16[160,512]{1,0:T(8,128)(2,1)S(1)}, u32[]{:S(2)}, u32[]{:S(2)}) collective-permute-start(bf16[160,512]{1,0:T(8,128)(2,1)S(1)} %get-tuple-element.49), channel_id=1, source_target_pairs={{0,16},{8,24},{16,0},{24,8},{1,17},{9,25},{17,1},{25,9},{2,18},{10... | collective-permute-start | bytes 491528 | tf_op jit(solution)/shard_map/ppermute | solution.py:351
  50.5 0.4 collective-permute-start.16
  51.0 3.6 %collective-permute-done.14.refs_2_ = bf16[160,512]{1,0:T(8,128)(2,1)S(1)} collective-permute-done((bf16[160,512]{1,0:T(8,128)(2,1)S(1)}, bf16[160,512]{1,0:T(8,128)(2,1)S(1)}, u32[]{:S(2)}, u32[]{:S(2)}) %collective-permute-start.14) | collective-permute-done | bytes 163872 | tf_op jit(solution)/shard_map/ppermute | solution.py:351
  54.6 3.9 %collective-permute-done.15.refs_3_ = bf16[160,512]{1,0:T(8,128)(2,1)S(1)} collective-permute-done((bf16[160,512]{1,0:T(8,128)(2,1)S(1)}, bf16[160,512]{1,0:T(8,128)(2,1)S(1)}, u32[]{:S(2)}, u32[]{:S(2)}) %collective-permute-start.15) | collective-permute-done | bytes 163872 | tf_op jit(solution)/shard_map/ppermute | solution.py:351
  58.5 1.6 %gated_traces.1 = f32[8,160,256]{2,1,0:T(8,128)} custom-call(s32[160,256]{1,0:T(8,128)S(1)} %copy-done.2, bf16[160,512]{1,0:T(8,128)(2,1)S(1)} %get-tuple-element.47.refs_1_, bf16[160,512]{1,0:T(8,128)(2,1)S(1)} %collective-permute-done.14.refs_2_, bf16[160,512]{1,0:T(8,128)(2,1)S(1)} %collective-permute-done.15.refs_3_, ...), custom_call_target="tpu_custom_call" | custom-call | tf_op jit(solution)/shard_map/gated_traces/pallas_call | solution.py:338
  (20 shorter events, 0.2 us)
Async XLA Ops:
  2.4 9.8 %collective-permute-start.1 = (bf16[96,512]{1,0:T(8,128)(2,1)S(1)}, bf16[96,512]{1,0:T(8,128)(2,1)S(1)}, u32[]{:S(2)}, u32[]{:S(2)}) collective-permute-start(bf16[96,512]{1,0:T(8,128)(2,1)S(1)} %get-tuple-element.32), channel_id=1, source_target_pairs={{0,7},{1,6},{2,5},{3,4},{4,3},{5,2},{6,1},{7,0},{8,15},{9,14},{10,... | collective-permute-start | bytes 294920 | tf_op jit(solution)/shard_map/ppermute | solution.py:351
  7.0 8.8 %collective-permute-start = (bf16[96,512]{1,0:T(8,128)(2,1)S(1)}, bf16[96,512]{1,0:T(8,128)(2,1)S(1)}, u32[]{:S(2)}, u32[]{:S(2)}) collective-permute-start(bf16[96,512]{1,0:T(8,128)(2,1)S(1)} %get-tuple-element.28.refs_3_), channel_id=1, source_target_pairs={{0,6},{1,7},{2,4},{3,5},{4,2},{5,3},{6,0},{7,1},{8,14},{9,15},{10,... | collective-permute-start | bytes 294920 | tf_op jit(solution)/shard_map/ppermute | solution.py:351
  10.0 11.2 %collective-permute-start.3 = (bf16[96,512]{1,0:T(8,128)(2,1)S(1)}, bf16[96,512]{1,0:T(8,128)(2,1)S(1)}, u32[]{:S(2)}, u32[]{:S(2)}) collective-permute-start(bf16[96,512]{1,0:T(8,128)(2,1)S(1)} %get-tuple-element.33), channel_id=1, source_target_pairs={{0,3},{1,2},{2,1},{3,0},{4,7},{5,6},{6,5},{7,4},{8,11},{9,10},{10,... | collective-permute-start | bytes 294920 | tf_op jit(solution)/shard_map/ppermute | solution.py:351
  10.0 11.1 %collective-permute-start.4 = (bf16[96,512]{1,0:T(8,128)(2,1)S(1)}, bf16[96,512]{1,0:T(8,128)(2,1)S(1)}, u32[]{:S(2)}, u32[]{:S(2)}) collective-permute-start(bf16[96,512]{1,0:T(8,128)(2,1)S(1)} %get-tuple-element.35), channel_id=1, source_target_pairs={{0,1},{1,0},{2,3},{3,2},{4,5},{5,4},{6,7},{7,6},{8,9},{9,8},{10,11... | collective-permute-start | bytes 294920 | tf_op jit(solution)/shard_map/ppermute | solution.py:351
  10.1 11.0 %collective-permute-start.2 = (bf16[96,512]{1,0:T(8,128)(2,1)S(1)}, bf16[96,512]{1,0:T(8,128)(2,1)S(1)}, u32[]{:S(2)}, u32[]{:S(2)}) collective-permute-start(bf16[96,512]{1,0:T(8,128)(2,1)S(1)} %get-tuple-element.29.refs_1_), channel_id=1, source_target_pairs={{0,2},{1,3},{2,0},{3,1},{4,6},{5,7},{6,4},{7,5},{8,10},{9,11},{10,... | collective-permute-start | bytes 294920 | tf_op jit(solution)/shard_map/ppermute | solution.py:351
  12.2 11.1 %collective-permute-start.5 = (bf16[96,512]{1,0:T(8,128)(2,1)S(1)}, bf16[96,512]{1,0:T(8,128)(2,1)S(1)}, u32[]{:S(2)}, u32[]{:S(2)}) collective-permute-start(bf16[96,512]{1,0:T(8,128)(2,1)S(1)} %get-tuple-element.36), channel_id=1, source_target_pairs={{0,4},{1,5},{2,6},{3,7},{4,0},{5,1},{6,2},{7,3},{8,12},{9,13},{10,... | collective-permute-start | bytes 294920 | tf_op jit(solution)/shard_map/ppermute | solution.py:351
  15.8 9.3 %collective-permute-start.6 = (bf16[96,512]{1,0:T(8,128)(2,1)S(1)}, bf16[96,512]{1,0:T(8,128)(2,1)S(1)}, u32[]{:S(2)}, u32[]{:S(2)}) collective-permute-start(bf16[96,512]{1,0:T(8,128)(2,1)S(1)} %get-tuple-element.37), channel_id=1, source_target_pairs={{0,5},{1,4},{2,7},{3,6},{4,1},{5,0},{6,3},{7,2},{8,13},{9,12},{10,... | collective-permute-start | bytes 294920 | tf_op jit(solution)/shard_map/ppermute | solution.py:351
  21.1 4.0 %copy-start = (bf16[4,640,384]{2,1,0:T(8,128)(2,1)}, bf16[4,640,384]{2,1,0:T(8,128)(2,1)S(1)}, u32[]{:S(2)}) copy-start(bf16[4,640,384]{2,1,0:T(8,128)(2,1)S(1)} %get-tuple-element.31.refs_0_.refs_2_) | copy-start | bytes 5898244
  21.1 4.0 %copy-start.1 = (bf16[1,2,640,256]{3,2,1,0:T(8,128)(2,1)S(1)}, bf16[1,2,640,256]{3,2,1,0:T(8,128)(2,1)}, u32[]{:S(2)}) copy-start(bf16[1,2,640,256]{3,2,1,0:T(8,128)(2,1)} %param.7) | copy-start | bytes 1966084
  21.1 4.0 %copy-start.3 = (s32[1,8,8]{2,1,0:T(8,128)S(1)}, s32[1,8,8]{2,1,0:T(8,128)}, u32[]{:S(2)}) copy-start(s32[1,8,8]{2,1,0:T(8,128)} %param.10) | copy-start | bytes 772
  27.9 6.9 %collective-permute-start.7 = (bf16[96,512]{1,0:T(8,128)(2,1)S(1)}, bf16[96,512]{1,0:T(8,128)(2,1)S(1)}, u32[]{:S(2)}, u32[]{:S(2)}) collective-permute-start(bf16[96,512]{1,0:T(8,128)(2,1)S(1)} %get-tuple-element.39), channel_id=1, source_target_pairs={{0,6},{1,7},{2,4},{3,5},{4,2},{5,3},{6,0},{7,1},{8,14},{9,15},{10,... | collective-permute-start | bytes 294920 | tf_op jit(solution)/shard_map/ppermute | solution.py:351
  29.7 6.9 %collective-permute-start.8 = (bf16[96,512]{1,0:T(8,128)(2,1)S(1)}, bf16[96,512]{1,0:T(8,128)(2,1)S(1)}, u32[]{:S(2)}, u32[]{:S(2)}) collective-permute-start(bf16[96,512]{1,0:T(8,128)(2,1)S(1)} %get-tuple-element.40), channel_id=1, source_target_pairs={{0,7},{1,6},{2,5},{3,4},{4,3},{5,2},{6,1},{7,0},{8,15},{9,14},{10,... | collective-permute-start | bytes 294920 | tf_op jit(solution)/shard_map/ppermute | solution.py:351
  32.5 9.2 %collective-permute-start.9 = (bf16[96,512]{1,0:T(8,128)(2,1)S(1)}, bf16[96,512]{1,0:T(8,128)(2,1)S(1)}, u32[]{:S(2)}, u32[]{:S(2)}) collective-permute-start(bf16[96,512]{1,0:T(8,128)(2,1)S(1)} %get-tuple-element.41), channel_id=1, source_target_pairs={{0,2},{1,3},{2,0},{3,1},{4,6},{5,7},{6,4},{7,5},{8,10},{9,11},{10,... | collective-permute-start | bytes 294920 | tf_op jit(solution)/shard_map/ppermute | solution.py:351
  32.6 10.7 %collective-permute-start.10 = (bf16[96,512]{1,0:T(8,128)(2,1)S(1)}, bf16[96,512]{1,0:T(8,128)(2,1)S(1)}, u32[]{:S(2)}, u32[]{:S(2)}) collective-permute-start(bf16[96,512]{1,0:T(8,128)(2,1)S(1)} %get-tuple-element.42), channel_id=1, source_target_pairs={{0,3},{1,2},{2,1},{3,0},{4,7},{5,6},{6,5},{7,4},{8,11},{9,10},{10,... | collective-permute-start | bytes 294920 | tf_op jit(solution)/shard_map/ppermute | solution.py:351
  34.6 8.7 %collective-permute-start.11 = (bf16[96,512]{1,0:T(8,128)(2,1)S(1)}, bf16[96,512]{1,0:T(8,128)(2,1)S(1)}, u32[]{:S(2)}, u32[]{:S(2)}) collective-permute-start(bf16[96,512]{1,0:T(8,128)(2,1)S(1)} %get-tuple-element.44), channel_id=1, source_target_pairs={{0,1},{1,0},{2,3},{3,2},{4,5},{5,4},{6,7},{7,6},{8,9},{9,8},{10,11... | collective-permute-start | bytes 294920 | tf_op jit(solution)/shard_map/ppermute | solution.py:351
  34.7 9.8 %collective-permute-start.12 = (bf16[96,512]{1,0:T(8,128)(2,1)S(1)}, bf16[96,512]{1,0:T(8,128)(2,1)S(1)}, u32[]{:S(2)}, u32[]{:S(2)}) collective-permute-start(bf16[96,512]{1,0:T(8,128)(2,1)S(1)} %get-tuple-element.45), channel_id=1, source_target_pairs={{0,4},{1,5},{2,6},{3,7},{4,0},{5,1},{6,2},{7,3},{8,12},{9,13},{10,... | collective-permute-start | bytes 294920 | tf_op jit(solution)/shard_map/ppermute | solution.py:351
  36.6 10.2 %collective-permute-start.13 = (bf16[96,512]{1,0:T(8,128)(2,1)S(1)}, bf16[96,512]{1,0:T(8,128)(2,1)S(1)}, u32[]{:S(2)}, u32[]{:S(2)}) collective-permute-start(bf16[96,512]{1,0:T(8,128)(2,1)S(1)} %get-tuple-element.46), channel_id=1, source_target_pairs={{0,5},{1,4},{2,7},{3,6},{4,1},{5,0},{6,3},{7,2},{8,13},{9,12},{10,... | collective-permute-start | bytes 294920 | tf_op jit(solution)/shard_map/ppermute | solution.py:351
  44.5 13.9 %copy-start.2 = (s32[160,256]{1,0:T(8,128)S(1)}, s32[160,256]{1,0:T(8,128)}, u32[]{:S(2)}) copy-start(s32[160,256]{1,0:T(8,128)} %refs_0_.1) | copy-start | bytes 491524
  47.4 7.1 %collective-permute-start.14 = (bf16[160,512]{1,0:T(8,128)(2,1)S(1)}, bf16[160,512]{1,0:T(8,128)(2,1)S(1)}, u32[]{:S(2)}, u32[]{:S(2)}) collective-permute-start(bf16[160,512]{1,0:T(8,128)(2,1)S(1)} %get-tuple-element.48), channel_id=1, source_target_pairs={{0,8},{8,0},{16,24},{24,16},{1,9},{9,1},{17,25},{25,17},{2,10},{10... | collective-permute-start | bytes 491528 | tf_op jit(solution)/shard_map/ppermute | solution.py:351
  49.0 9.4 %collective-permute-start.15 = (bf16[160,512]{1,0:T(8,128)(2,1)S(1)}, bf16[160,512]{1,0:T(8,128)(2,1)S(1)}, u32[]{:S(2)}, u32[]{:S(2)}) collective-permute-start(bf16[160,512]{1,0:T(8,128)(2,1)S(1)} %get-tuple-element.49), channel_id=1, source_target_pairs={{0,16},{8,24},{16,0},{24,8},{1,17},{9,25},{17,1},{25,9},{2,18},{10... | collective-permute-start | bytes 491528 | tf_op jit(solution)/shard_map/ppermute | solution.py:351
  50.5 7.9 %collective-permute-start.16 = (bf16[160,512]{1,0:T(8,128)(2,1)S(1)}, bf16[160,512]{1,0:T(8,128)(2,1)S(1)}, u32[]{:S(2)}, u32[]{:S(2)}) collective-permute-start(bf16[160,512]{1,0:T(8,128)(2,1)S(1)} %get-tuple-element.50), channel_id=1, source_target_pairs={{0,24},{8,16},{16,8},{24,0},{1,25},{9,17},{17,9},{25,1},{2,26},{10... | collective-permute-start | bytes 491528 | tf_op jit(solution)/shard_map/ppermute | solution.py:351
where the time goes:
time: 60.3 us; the launch traced here: 60.1 us
  starting transfers between devices  24.3 us (40%)
  Pallas kernels  20.2 us (33%)
  waiting for transfers between devices  15.4 us (26%)
    ppermute x17, starting transfers between devices, send(): return lax.ppermute(block, axis, [(i, i ^ k) for i in range(count)])  24.3 us
    ppermute x17, waiting for transfers between devices, send(): return lax.ppermute(block, axis, [(i, i ^ k) for i in range(count)])  15.4 us
    pallas_call x2, Pallas kernels, prepare(): pl.pallas_call(functools.partial(prepare_kernel, want_rows), out_shape=ou...  6.77 us
    pallas_call x2, Pallas kernels, coeff_blocks(): pl.pallas_call(functools.partial(coeff_kernel, ks, group), out_shape=[jax...  4.72 us
    pallas_call x1, Pallas kernels, residual_blocks(): pl.pallas_call(functools.partial(residual_kernel, base, ks), out_shape=ou...  2.75 us
    pallas_call x2, Pallas kernels, partial_sum(): pl.pallas_call(functools.partial(partial_kernel, bases), out_shape=jax.Sh...  2.44 us
    pallas_call x1, Pallas kernels, gated_traces(): pl.pallas_call(functools.partial(traces_kernel, freqs), out_shape=jax.Sha...  1.64 us
    pallas_call x1, Pallas kernels, adjoint_blocks(): pl.pallas_call(functools.partial(adjoint_kernel, ks), out_shape=[jax.Shap...  1.31 us
  transfers between devices with their start and end apart: 17, of which 7 were waited for; matrix products, arithmetic and copies ran while one was open for 0% of the time, Pallas kernels for 21%

commit v1 on v0

v1 whole, which is shorter than its diff:
```python
import functools
import math

import jax
import jax.numpy as jnp
from jax import lax
from jax.experimental import pallas as pl
from jax.experimental.pallas import tpu as pltpu
from jax.sharding import PartitionSpec as P


RMAX = 96
LANES = 128
BF16 = jnp.bfloat16
F32 = jnp.float32
VMEM = pl.BlockSpec(memory_space=pltpu.VMEM)
SMEM = pl.BlockSpec(memory_space=pltpu.SMEM)
ANY = pl.BlockSpec(memory_space=pl.ANY)
HBM = pl.BlockSpec(memory_space=pltpu.MemorySpace.HBM)


def params():
    return pltpu.CompilerParams(vmem_limit_bytes=48 * 1024 * 1024)


def masked(value, rank):
    level = lax.broadcasted_iota(jnp.int32, value.shape, 0)
    return jnp.where(level < rank, value, 0.0).astype(BF16)


def cost(flops):
    return pl.CostEstimate(flops=flops, bytes_accessed=10**7, transcendentals=0)


def coeff_outputs(ks, rank_ref, factors, wide, product, outs):
    me = lax.axis_index("tile")
    stations = factors.shape[3]
    left = factors[...].reshape(len(ks) * 2 * RMAX, stations)
    result = jnp.dot(left, wide[...], preferred_element_type=F32)
    parts = wide.shape[1] // LANES
    half = parts // 2
    for j in range(parts):
        product[j] = result[:, j * LANES : (j + 1) * LANES]
    for i, k in enumerate(ks):
        rank = rank_ref[me ^ k, me]
        base = i * 2 * RMAX
        even = [product[j, pl.ds(base, RMAX, stride=2), :] for j in range(parts)]
        odd = [product[j, pl.ds(base + 1, RMAX, stride=2), :] for j in range(parts)]
        for j in range(half):
            real = masked(even[j] + odd[half + j], rank)
            imag = masked(even[half + j] - odd[j], rank)
            outs[i][:, j * LANES : (j + 1) * LANES] = real
            outs[i][:, (half + j) * LANES : (half + j + 1) * LANES] = imag


def coeff_far_kernel(far, near, *refs):
    rank_hbm, v_hbm, x_hbm = refs[:3]
    outs = refs[3 : 3 + len(far)]
    wide, near_factors = refs[3 + len(far) : 5 + len(far)]
    rank_ref, factors, field, product, sems, near_sems, field_sem, rank_sem = refs[5 + len(far) :]
    me = lax.axis_index("tile")
    virtual = field.shape[2]
    rank_copy = pltpu.make_async_copy(rank_hbm, rank_ref, rank_sem)
    field_copy = pltpu.make_async_copy(x_hbm, field, field_sem)
    far_copies = [
        pltpu.make_async_copy(v_hbm.at[me ^ k, pl.ds(0, RMAX)], factors.at[i], sems.at[i])
        for i, k in enumerate(far)
    ]
    near_copies = [
        pltpu.make_async_copy(
            v_hbm.at[me ^ k, pl.ds(0, RMAX)], near_factors.at[i], near_sems.at[i]
        )
        for i, k in enumerate(near)
    ]
    field_copy.start()
    for copy in far_copies:
        copy.start()
    rank_copy.start()
    for copy in near_copies:
        copy.start()
    field_copy.wait()
    wide[:, :virtual] = field[0]
    wide[:, virtual:] = field[1]
    rank_copy.wait()
    for copy in far_copies:
        copy.wait()
    coeff_outputs(far, rank_ref, factors, wide, product, outs)
    for copy in near_copies:
        copy.wait()


def coeff_far(ranks, v, x, far, near):
    stations, virtual = x.shape[1], x.shape[2]
    outs = [jax.ShapeDtypeStruct((RMAX, 2 * virtual), BF16) for _ in far]
    outs.append(jax.ShapeDtypeStruct((stations, 2 * virtual), BF16))
    outs.append(jax.ShapeDtypeStruct((len(near), RMAX, 2, stations), BF16))
    return pl.pallas_call(
        functools.partial(coeff_far_kernel, far, near),
        out_shape=outs,
        in_specs=[HBM, HBM, HBM],
        out_specs=[VMEM for _ in outs],
        scratch_shapes=[
            pltpu.SMEM(ranks.shape, jnp.int32),
            pltpu.VMEM((len(far), RMAX, 2, stations), BF16),
            pltpu.VMEM((2, stations, virtual), BF16),
            pltpu.VMEM((2 * virtual // LANES, len(far) * 2 * RMAX, LANES), F32),
            pltpu.SemaphoreType.DMA((len(far),)),
            pltpu.SemaphoreType.DMA((len(near),)),
            pltpu.SemaphoreType.DMA,
            pltpu.SemaphoreType.DMA,
        ],
        compiler_params=params(),
        cost_estimate=cost(10**9),
        name="coeff_far",
    )(ranks, v, x)


def coeff_near_kernel(near, *refs):
    rank_ref, wide, factors = refs[:3]
    coeff_outputs(near, rank_ref, factors, wide, refs[-1], refs[3 : 3 + len(near)])


def coeff_near(ranks, wide, factors, near):
    width = wide.shape[1]
    return pl.pallas_call(
        functools.partial(coeff_near_kernel, near),
        out_shape=[jax.ShapeDtypeStruct((RMAX, width), BF16) for _ in near],
        in_specs=[SMEM, VMEM, VMEM],
        out_specs=[VMEM for _ in near],
        scratch_shapes=[pltpu.VMEM((width // LANES, len(near) * 2 * RMAX, LANES), F32)],
        compiler_params=params(),
        cost_estimate=cost(10**9),
        name="coeff_near",
    )(ranks, wide, factors)


def prepare_kernel(want_rows, *refs):
    w_hbm, _ = refs[:2]
    turned_ref = refs[2]
    if want_rows:
        rows_ref = refs[3]
        factors, spread, paired, sems = refs[4:]
    else:
        rows_ref = None
        factors, spread, paired, sems = refs[3:]
    me = lax.axis_index("tile")
    count = factors.shape[0]
    stations = factors.shape[3]
    columns = stations // LANES
    copies = [
        pltpu.make_async_copy(w_hbm.at[me ^ k, pl.ds(0, RMAX)], factors.at[k], sems.at[k])
        for k in range(count)
    ]
    for copy in copies:
        copy.start()
    for k in range(count):
        copies[k].wait()
        flat = factors[k].reshape(2 * RMAX, stations).astype(F32)
        for j in range(columns):
            spread[j] = flat[:, j * LANES : (j + 1) * LANES]
        for p in range(2):
            for j in range(columns):
                piece = spread[j, pl.ds(p, RMAX, stride=2), :].astype(BF16)
                row = (2 * p + k % 2) * RMAX
                paired[row : row + RMAX, j * LANES : (j + 1) * LANES] = piece
                if rows_ref is not None:
                    column = p * stations + j * LANES
                    rows_ref[k * RMAX : (k + 1) * RMAX, column : column + LANES] = piece
        if k % 2:
            for i in range(4 * RMAX // LANES):
                block = paired[i * LANES : (i + 1) * LANES, :]
                turned_ref[k // 2, :, i * LANES : (i + 1) * LANES] = block.T


def prepare(w, after, want_rows):
    count, _, _, stations = w.shape
    outs = [jax.ShapeDtypeStruct((count // 2, stations, 4 * RMAX), BF16)]
    if want_rows:
        outs.append(jax.ShapeDtypeStruct((count * RMAX, 2 * stations), BF16))
    return pl.pallas_call(
        functools.partial(prepare_kernel, want_rows),
        out_shape=outs,
        in_specs=[HBM, ANY],
        out_specs=[VMEM for _ in outs],
        scratch_shapes=[
            pltpu.VMEM((count, RMAX, 2, stations), BF16),
            pltpu.VMEM((stations // LANES, 2 * RMAX, LANES), F32),
            pltpu.VMEM((4 * RMAX, stations), BF16),
            pltpu.SemaphoreType.DMA((count,)),
        ],
        compiler_params=params(),
        cost_estimate=cost(10**9),
        name="prepare",
    )(w, after)


def apply_pairs(bases, blocks, turned_ref):
    virtual = blocks[0].shape[1] // 2
    total = None
    for i, base in enumerate(bases):
        pair = [blocks[2 * i][...], blocks[2 * i + 1][...]]
        turned = [jnp.concatenate([-b[:, virtual:], b[:, :virtual]], axis=1) for b in pair]
        stack = jnp.concatenate(pair + turned, axis=0)
        term = jnp.dot(turned_ref[base // 2], stack, preferred_element_type=F32)
        total = term if total is None else total + term
    return total


def partial_kernel(bases, *refs):
    turned_ref = refs[0]
    out_ref = refs[-1]
    out_ref[...] = apply_pairs(bases, refs[1:-1], turned_ref)


def partial_sum(turned, bases, blocks):
    stations = turned.shape[1]
    width = blocks[0].shape[1]
    return pl.pallas_call(
        functools.partial(partial_kernel, bases),
        out_shape=jax.ShapeDtypeStruct((stations, width), F32),
        in_specs=[VMEM] * (1 + len(blocks)),
        out_specs=VMEM,
        compiler_params=params(),
        cost_estimate=cost(10**9),
        name="partial_sum",
    )(turned, *blocks)


def adjoint_outputs(ks, rank_ref, rows_ref, stacked, outs):
    me = lax.axis_index("tile")
    low = min(ks)
    rows = rows_ref[low * RMAX : (low + len(ks)) * RMAX, :]
    product = jnp.dot(rows, stacked[...], preferred_element_type=F32)
    for i, k in enumerate(ks):
        block = product[(k - low) * RMAX : (k - low + 1) * RMAX, :]
        outs[i][...] = masked(block, rank_ref[me, me ^ k])


def residual_kernel(base, ks, *refs):
    rank_ref, rows_ref, turned_ref, data_ref, partial_ref = refs[:5]
    blocks = refs[5:7]
    outs = refs[7 : 7 + len(ks)]
    stacked = refs[7 + len(ks)]
    stations, virtual = data_ref.shape[1], data_ref.shape[2]
    predicted = partial_ref[...] + apply_pairs((base,), blocks, turned_ref)
    real = (predicted[:, :virtual] - data_ref[0].astype(F32)).astype(BF16)
    imag = (predicted[:, virtual:] - data_ref[1].astype(F32)).astype(BF16)
    stacked[:stations, :virtual] = real
    stacked[:stations, virtual:] = imag
    stacked[stations:, :virtual] = imag
    stacked[stations:, virtual:] = -real
    adjoint_outputs(ks, rank_ref, rows_ref, stacked, outs)


def residual_blocks(ranks, rows, turned, data, partial, base, blocks, ks):
    stations, virtual = data.shape[1], data.shape[2]
    outs = [jax.ShapeDtypeStruct((RMAX, 2 * virtual), BF16) for _ in ks]
    outs.append(jax.ShapeDtypeStruct((2 * stations, 2 * virtual), BF16))
    return pl.pallas_call(
        functools.partial(residual_kernel, base, ks),
        out_shape=outs,
        in_specs=[SMEM] + [VMEM] * 6,
        out_specs=[VMEM for _ in outs],
        compiler_params=params(),
        cost_estimate=cost(10**9),
        name="residual_blocks",
    )(ranks, rows, turned, data, partial, *blocks)


def adjoint_kernel(ks, *refs):
    adjoint_outputs(ks, *refs[:3], refs[3:])


def adjoint_blocks(ranks, rows, stacked, ks):
    width = stacked.shape[1]
    return pl.pallas_call(
        functools.partial(adjoint_kernel, ks),
        out_shape=[jax.ShapeDtypeStruct((RMAX, width), BF16) for _ in ks],
        in_specs=[SMEM, VMEM, VMEM],
        out_specs=[VMEM for _ in ks],
        compiler_params=params(),
        cost_estimate=cost(10**9),
        name="adjoint_blocks",
    )(ranks, rows, stacked)


def spectrum_kernel(base, freqs, *refs):
    turned_ref, partial_ref = refs[:2]
    outs = refs[4 : 4 + freqs]
    spectrum = refs[4 + freqs]
    mine = lax.axis_index("freq")
    spectrum[...] = partial_ref[...] + apply_pairs((base,), refs[2:4], turned_ref)
    share = outs[0].shape[0]
    for k in range(freqs):
        rows = pl.ds(pl.multiple_of((mine ^ k) * share, 8), share)
        outs[k][...] = spectrum[rows, :].astype(BF16)


def spectrum_blocks(turned, partial, base, blocks, freqs):
    stations, width = partial.shape
    return pl.pallas_call(
        functools.partial(spectrum_kernel, base, freqs),
        out_shape=[jax.ShapeDtypeStruct((stations // freqs, width), BF16) for _ in range(freqs)],
        in_specs=[VMEM] * 4,
        out_specs=[VMEM] * freqs,
        scratch_shapes=[pltpu.VMEM((stations, width), F32)],
        compiler_params=params(),
        cost_estimate=cost(10**9),
        name="spectrum_blocks",
    )(turned, partial, *blocks)


def traces_kernel(freqs, *refs):
    onset_ref = refs[0]
    blocks = refs[1 : 1 + freqs]
    out_hbm, gathered, traces, sems = refs[1 + freqs :]
    mine = lax.axis_index("freq")
    virtual = onset_ref.shape[1]
    for k in range(freqs):
        gathered[mine ^ k] = blocks[k][...]
    times = 2 * freqs
    scaling = 1.0 / math.sqrt(freqs)
    copies = [
        pltpu.make_async_copy(traces.at[t], out_hbm.at[t], sems.at[t]) for t in range(times)
    ]
    onset = onset_ref[...]
    for t in range(freqs):
        sums = [None, None]
        for f in range(freqs):
            turn = (f + 1) * t % times
            angle = 2.0 * math.pi * turn / times
            quarter = 4 * turn % times == 0
            for part, weight in ((0, math.cos(angle)), (1, -math.sin(angle))):
                if quarter:
                    weight = float(round(weight))
                if weight != 0.0:
                    value = gathered[f, :, part * virtual : (part + 1) * virtual]
                    term = value.astype(F32) * (weight * scaling)
                    old = sums[f % 2]
                    sums[f % 2] = term if old is None else old + term
        odd, even = sums
        traces[t] = jnp.where(t >= onset, even + odd, 0.0)
        copies[t].start()
        traces[t + freqs] = jnp.where(t + freqs >= onset, even - odd, 0.0)
        copies[t + freqs].start()
    for copy in copies:
        copy.wait()


def gated_traces(onset, blocks):
    freqs = len(blocks)
    share, virtual = onset.shape
    return pl.pallas_call(
        functools.partial(traces_kernel, freqs),
        out_shape=jax.ShapeDtypeStruct((2 * freqs, share, virtual), F32),
        in_specs=[VMEM] * (1 + freqs),
        out_specs=HBM,
        scratch_shapes=[
            pltpu.VMEM((freqs, share, 2 * virtual), BF16),
            pltpu.VMEM((2 * freqs, share, virtual), F32),
            pltpu.SemaphoreType.DMA((2 * freqs,)),
        ],
        compiler_params=params(),
        name="gated_traces",
    )(onset, *blocks)


def send(block, axis, k):
    count = lax.axis_size(axis)
    return lax.ppermute(block, axis, [(i, i ^ k) for i in range(count)])


def exchange(ks, blocks):
    return {k: send(b, "tile", k) if k else b for k, b in zip(ks, blocks)}


def pick(arrived, bases):
    return [arrived[base + b] for base in bases for b in range(2)]


def pair_bases(count):
    return list(range(count - 2, -1, -2))


def peer_order(count):
    bases = pair_bases(count)
    half = len(bases) // 2
    far = tuple(base + b for base in bases[:half] for b in range(2))
    near = tuple(base + b for base in bases[half:] for b in range(2))
    return far, near


def hbm(array):
    return pltpu.with_memory_space_constraint(array, pltpu.MemorySpace.HBM)


def body(x_field, data, u_bases, v_bases, ranks, onset):
    count = lax.axis_size("tile")
    freqs = lax.axis_size("freq")
    table = ranks[0]
    u = hbm(u_bases[0, 0])
    v = hbm(v_bases[0, :, 0])
    x = hbm(x_field[0])
    late = count // 2
    early = tuple(base for base in pair_bases(count) if base != late)
    far, near = peer_order(count)
    *blocks, wide, near_factors = coeff_far(hbm(table), v, x, far, near)
    arrived = exchange(far, blocks)
    blocks = coeff_near(table, wide, near_factors, near)
    arrived |= exchange(near, blocks)
    u_turned, u_rows = prepare(u, blocks[0], True)
    partial = partial_sum(u_turned, early, pick(arrived, early))
    *blocks, stacked = residual_blocks(
        table, u_rows, u_turned, data[0], partial, late, pick(arrived, (late,)), far
    )
    returned = exchange(far, blocks)
    blocks = adjoint_blocks(table, u_rows, stacked, near)
    returned |= exchange(near, blocks)
    (v_turned,) = prepare(v, stacked, False)
    partial = partial_sum(v_turned, early, pick(returned, early))
    spectrum = spectrum_blocks(v_turned, partial, late, pick(returned, (late,)), freqs)
    spectra = [send(block, "freq", k) if k else block for k, block in enumerate(spectrum)]
    return gated_traces(onset, spectra)


def solution(mesh):
    in_specs = (
        P("freq", None, "tile", None),
        P("freq", None, "tile", None),
        P("freq", "tile", None, None, None, None),
        P("freq", None, "tile", None, None, None),
        P("freq", None, None),
        P(("tile", "freq"), None),
    )
    out_specs = P(None, ("tile", "freq"), None)

    return jax.shard_map(
        body, mesh=mesh, in_specs=in_specs, out_specs=out_specs, check_vma=False
    )
```

time: 60.3 us -> 63 us (1.045)
  waiting for transfers between devices: 15.4 us -> 22.3 us
  starting transfers between devices: 24.3 us -> 21.1 us
  Pallas kernels: 20.2 us -> 19.2 us
    ppermute x17, waiting for transfers between devices: 15.4 us -> 22.3 us  [send(): return lax.ppermute(block, axis, [(i, i ^ k) for i in range(count)])]
    ppermute x17, starting transfers between devices: 24.3 us -> 21.1 us  [send(): return lax.ppermute(block, axis, [(i, i ^ k) for i in range(count)])]
  transfers between devices with their start and end apart: 17 -> 17, of which waited for: 7 -> 10; matrix products, arithmetic and copies ran while one was open for 0% -> 0% of each run, Pallas kernels for 21% -> 17%
where the time goes in v1:
time: 63 us; the launch traced here: 62.8 us
  waiting for transfers between devices  22.3 us (35%)
  starting transfers between devices  21.1 us (33%)
  Pallas kernels  19.2 us (30%)
    ppermute x17, waiting for transfers between devices, send(): return lax.ppermute(block, axis, [(i, i ^ k) for i in range(count)])  22.3 us
    ppermute x17, starting transfers between devices, send(): return lax.ppermute(block, axis, [(i, i ^ k) for i in range(count)])  21.1 us
    pallas_call x2, Pallas kernels, prepare(): pl.pallas_call(functools.partial(prepare_kernel, want_rows), out_shape=ou...  6.77 us
    pallas_call x1, Pallas kernels, coeff_far(): pl.pallas_call(functools.partial(coeff_far_kernel, far, near), out_shape=...  2.75 us
    pallas_call x1, Pallas kernels, residual_blocks(): pl.pallas_call(functools.partial(residual_kernel, base, ks), out_shape=ou...  2.63 us
    pallas_call x2, Pallas kernels, partial_sum(): pl.pallas_call(functools.partial(partial_kernel, bases), out_shape=jax.Sh...  2.35 us
    pallas_call x1, Pallas kernels, coeff_near(): pl.pallas_call(functools.partial(coeff_near_kernel, near), out_shape=[jax...  1.48 us
    pallas_call x1, Pallas kernels, gated_traces(): pl.pallas_call(functools.partial(traces_kernel, freqs), out_shape=jax.Sha...  1.34 us
  transfers between devices with their start and end apart: 17, of which 10 were waited for; matrix products, arithmetic and copies ran while one was open for 0% of the time, Pallas kernels for 17%

profile of v1, /device:TPU:0, one launch (start us, length us, event | category | flops | bytes accessed | tf_op | source)
XLA Modules:
  0.0 62.8 jit_solution(15429632029835351071)
XLA Ops:
  0.0 2.8 %coeff_far.1 = (bf16[96,512]{1,0:T(8,128)(2,1)S(1)}, bf16[96,512]{1,0:T(8,128)(2,1)S(1)}, bf16[96,512]{1,0:T(8,128)(2,1)S(1)}, bf16[96,512]{1,0:T(8,128)(2,1)S(1...) custom-call(s32[8,8]{1,0:T(8,128)} %bitcast.6, bf16[8,128,2,640]{3,2,1,0:T(2,128)(2,1)} %bitcast.10, ...), custom_call_target="tpu_custom_call" | custom-call | flops 1000000000 | bytes 10000000 | tf_op jit(solution)/shard_map/coeff_far/pallas_call | solution.py:97
  2.8 1.5 %coeff_near.1 = (bf16[96,512]{1,0:T(8,128)(2,1)S(1)}, bf16[96,512]{1,0:T(8,128)(2,1)S(1)}, bf16[96,512]{1,0:T(8,128)(2,1)S(1)}, bf16[96,512]{1,0:T(8,128)(2,1)S(1)}) custom-call(s32[8,8]{1,0:T(8,128)S(1)} %bitcast.7, bf16[640,512]{1,0:T(8,128)(2,1)S(1)} %get-tuple-element.30.refs_1_, bf16[4,96,2,640]{3,2,1,0:T(2,128)(2,1)S(1)} %get-tuple-element.31.refs_2_), custom_call_target="tpu_custom_call" | custom-call | flops 1000000000 | bytes 10000000 | tf_op jit(solution)/shard_map/coeff_near/pallas_call | solution.py:125
  4.3 2.6 %collective-permute-start.3 = (bf16[96,512]{1,0:T(8,128)(2,1)S(1)}, bf16[96,512]{1,0:T(8,128)(2,1)S(1)}, u32[]{:S(2)}, u32[]{:S(2)}) collective-permute-start(bf16[96,512]{1,0:T(8,128)(2,1)S(1)} %get-tuple-element.37), channel_id=1, source_target_pairs={{0,3},{1,2},{2,1},{3,0},{4,7},{5,6},{6,5},{7,4},{8,11},{9,10},{10,... | collective-permute-start | bytes 294920 | tf_op jit(solution)/shard_map/ppermute | solution.py:370
  6.8 0.7 %collective-permute-start.4 = (bf16[96,512]{1,0:T(8,128)(2,1)S(1)}, bf16[96,512]{1,0:T(8,128)(2,1)S(1)}, u32[]{:S(2)}, u32[]{:S(2)}) collective-permute-start(bf16[96,512]{1,0:T(8,128)(2,1)S(1)} %get-tuple-element.39), channel_id=1, source_target_pairs={{0,1},{1,0},{2,3},{3,2},{4,5},{5,4},{6,7},{7,6},{8,9},{9,8},{10,11... | collective-permute-start | bytes 294920 | tf_op jit(solution)/shard_map/ppermute | solution.py:370
  7.5 4.0 %collective-permute-start = (bf16[96,512]{1,0:T(8,128)(2,1)S(1)}, bf16[96,512]{1,0:T(8,128)(2,1)S(1)}, u32[]{:S(2)}, u32[]{:S(2)}) collective-permute-start(bf16[96,512]{1,0:T(8,128)(2,1)S(1)} %get-tuple-element.35), channel_id=1, source_target_pairs={{0,6},{1,7},{2,4},{3,5},{4,2},{5,3},{6,0},{7,1},{8,14},{9,15},{10,... | collective-permute-start | bytes 294920 | tf_op jit(solution)/shard_map/ppermute | solution.py:370
  11.6 1.8 %collective-permute-start.5 = (bf16[96,512]{1,0:T(8,128)(2,1)S(1)}, bf16[96,512]{1,0:T(8,128)(2,1)S(1)}, u32[]{:S(2)}, u32[]{:S(2)}) collective-permute-start(bf16[96,512]{1,0:T(8,128)(2,1)S(1)} %get-tuple-element.40), channel_id=1, source_target_pairs={{0,4},{1,5},{2,6},{3,7},{4,0},{5,1},{6,2},{7,3},{8,12},{9,13},{10,... | collective-permute-start | bytes 294920 | tf_op jit(solution)/shard_map/ppermute | solution.py:370
  13.3 0.6 collective-permute-start.6
  13.9 3.5 %prepare.2 = (bf16[4,640,384]{2,1,0:T(8,128)(2,1)S(1)}, bf16[768,1280]{1,0:T(8,128)(2,1)S(1)}) custom-call(bf16[8,128,2,640]{3,2,1,0:T(2,128)(2,1)} %bitcast.12, bf16[96,512]{1,0:T(8,128)(2,1)S(1)} %get-tuple-element.32.refs_1_), custom_call_target="tpu_custom_call" | custom-call | flops 1000000000 | bytes 10000000 | tf_op jit(solution)/shard_map/prepare/pallas_call | solution.py:180
  17.4 1.7 %collective-permute-done.1.refs_2_ = bf16[96,512]{1,0:T(8,128)(2,1)S(1)} collective-permute-done((bf16[96,512]{1,0:T(8,128)(2,1)S(1)}, bf16[96,512]{1,0:T(8,128)(2,1)S(1)}, u32[]{:S(2)}, u32[]{:S(2)}) %collective-permute-start.1) | collective-permute-done | bytes 98336 | tf_op jit(solution)/shard_map/ppermute | solution.py:370
  19.2 1.2 %partial_sum.2.refs_4_ = f32[640,512]{1,0:T(8,128)S(1)} custom-call(bf16[4,640,384]{2,1,0:T(8,128)(2,1)S(1)} %get-tuple-element.34.refs_0_.refs_2_, bf16[96,512]{1,0:T(8,128)(2,1)S(1)} %collective-permute-done.refs_1_, bf16[96,512]{1,0:T(8,128)(2,1)S(1)} %collective-permute-done.1.refs_2_, bf16[96,512]{1,0:T(8,128)(2,1)S(1)} %collective-permute-done.2.refs_3_, ...), custom_call_target="tpu_custom_call" | custom-call | flops 1000000000 | bytes 10000000 | tf_op jit(solution)/shard_map/partial_sum/pallas_call | solution.py:218
  20.3 5.9 %collective-permute-done.5.refs_5_ = bf16[96,512]{1,0:T(8,128)(2,1)S(1)} collective-permute-done((bf16[96,512]{1,0:T(8,128)(2,1)S(1)}, bf16[96,512]{1,0:T(8,128)(2,1)S(1)}, u32[]{:S(2)}, u32[]{:S(2)}) %collective-permute-start.5) | collective-permute-done | bytes 98336 | tf_op jit(solution)/shard_map/ppermute | solution.py:370
  26.3 2.0 %collective-permute-done.6.refs_6_ = bf16[96,512]{1,0:T(8,128)(2,1)S(1)} collective-permute-done((bf16[96,512]{1,0:T(8,128)(2,1)S(1)}, bf16[96,512]{1,0:T(8,128)(2,1)S(1)}, u32[]{:S(2)}, u32[]{:S(2)}) %collective-permute-start.6) | collective-permute-done | bytes 98336 | tf_op jit(solution)/shard_map/ppermute | solution.py:370
  28.3 2.6 %residual_blocks.1 = (bf16[96,512]{1,0:T(8,128)(2,1)S(1)}, bf16[96,512]{1,0:T(8,128)(2,1)S(1)}, bf16[96,512]{1,0:T(8,128)(2,1)S(1)}, bf16[96,512]{1,0:T(8,128)(2,1)S(1)}, bf16[1280,512]{1,0:T(8,128)(2,1)S(1)}) custom-call(s32[8,8]{1,0:T(8,128)S(1)} %bitcast.8, bf16[768,1280]{1,0:T(8,128)(2,1)S(1)} %get-tuple-element.33.refs_1_, ...), custom_call_target="tpu_custom_call" | custom-call | flops 1000000000 | bytes 10000000 | tf_op jit(solution)/shard_map/residual_blocks/pallas_call | solution.py:259
  30.9 1.4 %collective-permute-start.7 = (bf16[96,512]{1,0:T(8,128)(2,1)S(1)}, bf16[96,512]{1,0:T(8,128)(2,1)S(1)}, u32[]{:S(2)}, u32[]{:S(2)}) collective-permute-start(bf16[96,512]{1,0:T(8,128)(2,1)S(1)} %get-tuple-element.43), channel_id=1, source_target_pairs={{0,6},{1,7},{2,4},{3,5},{4,2},{5,3},{6,0},{7,1},{8,14},{9,15},{10,... | collective-permute-start | bytes 294920 | tf_op jit(solution)/shard_map/ppermute | solution.py:370
  32.3 1.9 %collective-permute-start.8 = (bf16[96,512]{1,0:T(8,128)(2,1)S(1)}, bf16[96,512]{1,0:T(8,128)(2,1)S(1)}, u32[]{:S(2)}, u32[]{:S(2)}) collective-permute-start(bf16[96,512]{1,0:T(8,128)(2,1)S(1)} %get-tuple-element.44), channel_id=1, source_target_pairs={{0,7},{1,6},{2,5},{3,4},{4,3},{5,2},{6,1},{7,0},{8,15},{9,14},{10,... | collective-permute-start | bytes 294920 | tf_op jit(solution)/shard_map/ppermute | solution.py:370
  34.2 1.3 %adjoint_blocks.1 = (bf16[96,512]{1,0:T(8,128)(2,1)S(1)}, bf16[96,512]{1,0:T(8,128)(2,1)S(1)}, bf16[96,512]{1,0:T(8,128)(2,1)S(1)}, bf16[96,512]{1,0:T(8,128)(2,1)S(1)}) custom-call(s32[8,8]{1,0:T(8,128)S(1)} %bitcast.9, bf16[768,1280]{1,0:T(8,128)(2,1)S(1)} %get-tuple-element.33.refs_1_, bf16[1280,512]{1,0:T(8,128)(2,1)S(1)} %get-tuple-element.42.refs_1_.refs_2_), custom_call_target="tpu_custom_call" | custom-call | flops 1000000000 | bytes 10000000 | tf_op jit(solution)/shard_map/adjoint_blocks/pallas_call | solution.py:276
  35.6 2.0 %collective-permute-start.10 = (bf16[96,512]{1,0:T(8,128)(2,1)S(1)}, bf16[96,512]{1,0:T(8,128)(2,1)S(1)}, u32[]{:S(2)}, u32[]{:S(2)}) collective-permute-start(bf16[96,512]{1,0:T(8,128)(2,1)S(1)} %get-tuple-element.46), channel_id=1, source_target_pairs={{0,3},{1,2},{2,1},{3,0},{4,7},{5,6},{6,5},{7,4},{8,11},{9,10},{10,... | collective-permute-start | bytes 294920 | tf_op jit(solution)/shard_map/ppermute | solution.py:370
  37.7 0.5 collective-permute-done.7.refs_1_
  38.5 0.9 %collective-permute-done.8.refs_2_ = bf16[96,512]{1,0:T(8,128)(2,1)S(1)} collective-permute-done((bf16[96,512]{1,0:T(8,128)(2,1)S(1)}, bf16[96,512]{1,0:T(8,128)(2,1)S(1)}, u32[]{:S(2)}, u32[]{:S(2)}) %collective-permute-start.8) | collective-permute-done | bytes 98336 | tf_op jit(solution)/shard_map/ppermute | solution.py:370
  39.3 2.0 %collective-permute-start.13 = (bf16[96,512]{1,0:T(8,128)(2,1)S(1)}, bf16[96,512]{1,0:T(8,128)(2,1)S(1)}, u32[]{:S(2)}, u32[]{:S(2)}) collective-permute-start(bf16[96,512]{1,0:T(8,128)(2,1)S(1)} %get-tuple-element.50), channel_id=1, source_target_pairs={{0,5},{1,4},{2,7},{3,6},{4,1},{5,0},{6,3},{7,2},{8,13},{9,12},{10,... | collective-permute-start | bytes 294920 | tf_op jit(solution)/shard_map/ppermute | solution.py:370
  41.4 3.3 %prepare.3.refs_0_ = bf16[4,640,384]{2,1,0:T(8,128)(2,1)S(1)} custom-call(bf16[8,128,2,640]{3,2,1,0:T(2,128)(2,1)} %bitcast.11, bf16[1280,512]{1,0:T(8,128)(2,1)S(1)} %get-tuple-element.42.refs_1_.refs_2_), custom_call_target="tpu_custom_call" | custom-call | flops 1000000000 | bytes 10000000 | tf_op jit(solution)/shard_map/prepare/pallas_call | solution.py:180
  44.7 1.7 %collective-permute-done.10.refs_4_ = bf16[96,512]{1,0:T(8,128)(2,1)S(1)} collective-permute-done((bf16[96,512]{1,0:T(8,128)(2,1)S(1)}, bf16[96,512]{1,0:T(8,128)(2,1)S(1)}, u32[]{:S(2)}, u32[]{:S(2)}) %collective-permute-start.10) | collective-permute-done | bytes 98336 | tf_op jit(solution)/shard_map/ppermute | solution.py:370
  46.4 1.2 %partial_sum.3.refs_1_ = f32[640,512]{1,0:T(8,128)S(1)} custom-call(bf16[4,640,384]{2,1,0:T(8,128)(2,1)S(1)} %prepare.3.refs_0_, bf16[96,512]{1,0:T(8,128)(2,1)S(1)} %collective-permute-done.7.refs_1_, bf16[96,512]{1,0:T(8,128)(2,1)S(1)} %collective-permute-done.8.refs_2_, bf16[96,512]{1,0:T(8,128)(2,1)S(1)} %collective-permute-done.9.refs_3_, ...), custom_call_target="tpu_custom_call" | custom-call | flops 1000000000 | bytes 10000000 | tf_op jit(solution)/shard_map/partial_sum/pallas_call | solution.py:218
  47.6 0.9 %collective-permute-done.12.refs_2_ = bf16[96,512]{1,0:T(8,128)(2,1)S(1)} collective-permute-done((bf16[96,512]{1,0:T(8,128)(2,1)S(1)}, bf16[96,512]{1,0:T(8,128)(2,1)S(1)}, u32[]{:S(2)}, u32[]{:S(2)}) %collective-permute-start.12) | collective-permute-done | bytes 98336 | tf_op jit(solution)/shard_map/ppermute | solution.py:370
  48.5 1.0 %collective-permute-done.13.refs_3_ = bf16[96,512]{1,0:T(8,128)(2,1)S(1)} collective-permute-done((bf16[96,512]{1,0:T(8,128)(2,1)S(1)}, bf16[96,512]{1,0:T(8,128)(2,1)S(1)}, u32[]{:S(2)}, u32[]{:S(2)}) %collective-permute-start.13) | collective-permute-done | bytes 98336 | tf_op jit(solution)/shard_map/ppermute | solution.py:370
  49.5 0.6 spectrum_blocks.1
  50.2 1.5 %collective-permute-start.14 = (bf16[160,512]{1,0:T(8,128)(2,1)S(1)}, bf16[160,512]{1,0:T(8,128)(2,1)S(1)}, u32[]{:S(2)}, u32[]{:S(2)}) collective-permute-start(bf16[160,512]{1,0:T(8,128)(2,1)S(1)} %get-tuple-element.52), channel_id=1, source_target_pairs={{0,8},{8,0},{16,24},{24,16},{1,9},{9,1},{17,25},{25,17},{2,10},{10... | collective-permute-start | bytes 491528 | tf_op jit(solution)/shard_map/ppermute | solution.py:370
  51.7 1.5 %collective-permute-start.15 = (bf16[160,512]{1,0:T(8,128)(2,1)S(1)}, bf16[160,512]{1,0:T(8,128)(2,1)S(1)}, u32[]{:S(2)}, u32[]{:S(2)}) collective-permute-start(bf16[160,512]{1,0:T(8,128)(2,1)S(1)} %get-tuple-element.53), channel_id=1, source_target_pairs={{0,16},{8,24},{16,0},{24,8},{1,17},{9,25},{17,1},{25,9},{2,18},{10... | collective-permute-start | bytes 491528 | tf_op jit(solution)/shard_map/ppermute | solution.py:370
  53.2 0.5 collective-permute-start.16
  53.7 3.6 %collective-permute-done.14.refs_2_ = bf16[160,512]{1,0:T(8,128)(2,1)S(1)} collective-permute-done((bf16[160,512]{1,0:T(8,128)(2,1)S(1)}, bf16[160,512]{1,0:T(8,128)(2,1)S(1)}, u32[]{:S(2)}, u32[]{:S(2)}) %collective-permute-start.14) | collective-permute-done | bytes 163872 | tf_op jit(solution)/shard_map/ppermute | solution.py:370
  57.3 4.1 %collective-permute-done.15.refs_3_ = bf16[160,512]{1,0:T(8,128)(2,1)S(1)} collective-permute-done((bf16[160,512]{1,0:T(8,128)(2,1)S(1)}, bf16[160,512]{1,0:T(8,128)(2,1)S(1)}, u32[]{:S(2)}, u32[]{:S(2)}) %collective-permute-start.15) | collective-permute-done | bytes 163872 | tf_op jit(solution)/shard_map/ppermute | solution.py:370
  61.4 1.3 %gated_traces.1 = f32[8,160,256]{2,1,0:T(8,128)} custom-call(s32[160,256]{1,0:T(8,128)S(1)} %copy-done.2, bf16[160,512]{1,0:T(8,128)(2,1)S(1)} %get-tuple-element.51.refs_1_, bf16[160,512]{1,0:T(8,128)(2,1)S(1)} %collective-permute-done.14.refs_2_, bf16[160,512]{1,0:T(8,128)(2,1)S(1)} %collective-permute-done.15.refs_3_, ...), custom_call_target="tpu_custom_call" | custom-call | tf_op jit(solution)/shard_map/gated_traces/pallas_call | solution.py:353
  (20 shorter events, 0.5 us)
Async XLA Ops:
  0.0 2.8 %copy-start.3 = (s32[1,8,8]{2,1,0:T(8,128)S(1)}, s32[1,8,8]{2,1,0:T(8,128)}, u32[]{:S(2)}) copy-start(s32[1,8,8]{2,1,0:T(8,128)} %param.10) | copy-start | bytes 772
  4.3 7.3 %collective-permute-start.3 = (bf16[96,512]{1,0:T(8,128)(2,1)S(1)}, bf16[96,512]{1,0:T(8,128)(2,1)S(1)}, u32[]{:S(2)}, u32[]{:S(2)}) collective-permute-start(bf16[96,512]{1,0:T(8,128)(2,1)S(1)} %get-tuple-element.37), channel_id=1, source_target_pairs={{0,3},{1,2},{2,1},{3,0},{4,7},{5,6},{6,5},{7,4},{8,11},{9,10},{10,... | collective-permute-start | bytes 294920 | tf_op jit(solution)/shard_map/ppermute | solution.py:370
  6.8 6.5 %collective-permute-start.4 = (bf16[96,512]{1,0:T(8,128)(2,1)S(1)}, bf16[96,512]{1,0:T(8,128)(2,1)S(1)}, u32[]{:S(2)}, u32[]{:S(2)}) collective-permute-start(bf16[96,512]{1,0:T(8,128)(2,1)S(1)} %get-tuple-element.39), channel_id=1, source_target_pairs={{0,1},{1,0},{2,3},{3,2},{4,5},{5,4},{6,7},{7,6},{8,9},{9,8},{10,11... | collective-permute-start | bytes 294920 | tf_op jit(solution)/shard_map/ppermute | solution.py:370
  7.5 9.9 %collective-permute-start.2 = (bf16[96,512]{1,0:T(8,128)(2,1)S(1)}, bf16[96,512]{1,0:T(8,128)(2,1)S(1)}, u32[]{:S(2)}, u32[]{:S(2)}) collective-permute-start(bf16[96,512]{1,0:T(8,128)(2,1)S(1)} %get-tuple-element.32.refs_1_), channel_id=1, source_target_pairs={{0,2},{1,3},{2,0},{3,1},{4,6},{5,7},{6,4},{7,5},{8,10},{9,11},{10,... | collective-permute-start | bytes 294920 | tf_op jit(solution)/shard_map/ppermute | solution.py:370
  7.5 9.9 %collective-permute-start = (bf16[96,512]{1,0:T(8,128)(2,1)S(1)}, bf16[96,512]{1,0:T(8,128)(2,1)S(1)}, u32[]{:S(2)}, u32[]{:S(2)}) collective-permute-start(bf16[96,512]{1,0:T(8,128)(2,1)S(1)} %get-tuple-element.35), channel_id=1, source_target_pairs={{0,6},{1,7},{2,4},{3,5},{4,2},{5,3},{6,0},{7,1},{8,14},{9,15},{10,... | collective-permute-start | bytes 294920 | tf_op jit(solution)/shard_map/ppermute | solution.py:370
  11.6 7.6 %collective-permute-start.1 = (bf16[96,512]{1,0:T(8,128)(2,1)S(1)}, bf16[96,512]{1,0:T(8,128)(2,1)S(1)}, u32[]{:S(2)}, u32[]{:S(2)}) collective-permute-start(bf16[96,512]{1,0:T(8,128)(2,1)S(1)} %get-tuple-element.36), channel_id=1, source_target_pairs={{0,7},{1,6},{2,5},{3,4},{4,3},{5,2},{6,1},{7,0},{8,15},{9,14},{10,... | collective-permute-start | bytes 294920 | tf_op jit(solution)/shard_map/ppermute | solution.py:370
  11.6 14.7 %collective-permute-start.5 = (bf16[96,512]{1,0:T(8,128)(2,1)S(1)}, bf16[96,512]{1,0:T(8,128)(2,1)S(1)}, u32[]{:S(2)}, u32[]{:S(2)}) collective-permute-start(bf16[96,512]{1,0:T(8,128)(2,1)S(1)} %get-tuple-element.40), channel_id=1, source_target_pairs={{0,4},{1,5},{2,6},{3,7},{4,0},{5,1},{6,2},{7,3},{8,12},{9,13},{10,... | collective-permute-start | bytes 294920 | tf_op jit(solution)/shard_map/ppermute | solution.py:370
  13.3 14.9 %collective-permute-start.6 = (bf16[96,512]{1,0:T(8,128)(2,1)S(1)}, bf16[96,512]{1,0:T(8,128)(2,1)S(1)}, u32[]{:S(2)}, u32[]{:S(2)}) collective-permute-start(bf16[96,512]{1,0:T(8,128)(2,1)S(1)} %get-tuple-element.41), channel_id=1, source_target_pairs={{0,5},{1,4},{2,7},{3,6},{4,1},{5,0},{6,3},{7,2},{8,13},{9,12},{10,... | collective-permute-start | bytes 294920 | tf_op jit(solution)/shard_map/ppermute | solution.py:370
  17.4 10.9 %copy-start = (bf16[4,640,384]{2,1,0:T(8,128)(2,1)}, bf16[4,640,384]{2,1,0:T(8,128)(2,1)S(1)}, u32[]{:S(2)}) copy-start(bf16[4,640,384]{2,1,0:T(8,128)(2,1)S(1)} %get-tuple-element.34.refs_0_.refs_2_) | copy-start | bytes 5898244
  17.4 10.9 %copy-start.1 = (bf16[1,2,640,256]{3,2,1,0:T(8,128)(2,1)S(1)}, bf16[1,2,640,256]{3,2,1,0:T(8,128)(2,1)}, u32[]{:S(2)}) copy-start(bf16[1,2,640,256]{3,2,1,0:T(8,128)(2,1)} %param.7) | copy-start | bytes 1966084
  30.9 7.3 %collective-permute-start.7 = (bf16[96,512]{1,0:T(8,128)(2,1)S(1)}, bf16[96,512]{1,0:T(8,128)(2,1)S(1)}, u32[]{:S(2)}, u32[]{:S(2)}) collective-permute-start(bf16[96,512]{1,0:T(8,128)(2,1)S(1)} %get-tuple-element.43), channel_id=1, source_target_pairs={{0,6},{1,7},{2,4},{3,5},{4,2},{5,3},{6,0},{7,1},{8,14},{9,15},{10,... | collective-permute-start | bytes 294920 | tf_op jit(solution)/shard_map/ppermute | solution.py:370
  32.3 7.0 %collective-permute-start.8 = (bf16[96,512]{1,0:T(8,128)(2,1)S(1)}, bf16[96,512]{1,0:T(8,128)(2,1)S(1)}, u32[]{:S(2)}, u32[]{:S(2)}) collective-permute-start(bf16[96,512]{1,0:T(8,128)(2,1)S(1)} %get-tuple-element.44), channel_id=1, source_target_pairs={{0,7},{1,6},{2,5},{3,4},{4,3},{5,2},{6,1},{7,0},{8,15},{9,14},{10,... | collective-permute-start | bytes 294920 | tf_op jit(solution)/shard_map/ppermute | solution.py:370
  35.5 9.2 %collective-permute-start.9 = (bf16[96,512]{1,0:T(8,128)(2,1)S(1)}, bf16[96,512]{1,0:T(8,128)(2,1)S(1)}, u32[]{:S(2)}, u32[]{:S(2)}) collective-permute-start(bf16[96,512]{1,0:T(8,128)(2,1)S(1)} %get-tuple-element.45), channel_id=1, source_target_pairs={{0,2},{1,3},{2,0},{3,1},{4,6},{5,7},{6,4},{7,5},{8,10},{9,11},{10,... | collective-permute-start | bytes 294920 | tf_op jit(solution)/shard_map/ppermute | solution.py:370
  35.6 10.8 %collective-permute-start.10 = (bf16[96,512]{1,0:T(8,128)(2,1)S(1)}, bf16[96,512]{1,0:T(8,128)(2,1)S(1)}, u32[]{:S(2)}, u32[]{:S(2)}) collective-permute-start(bf16[96,512]{1,0:T(8,128)(2,1)S(1)} %get-tuple-element.46), channel_id=1, source_target_pairs={{0,3},{1,2},{2,1},{3,0},{4,7},{5,6},{6,5},{7,4},{8,11},{9,10},{10,... | collective-permute-start | bytes 294920 | tf_op jit(solution)/shard_map/ppermute | solution.py:370
  37.6 8.8 %collective-permute-start.11 = (bf16[96,512]{1,0:T(8,128)(2,1)S(1)}, bf16[96,512]{1,0:T(8,128)(2,1)S(1)}, u32[]{:S(2)}, u32[]{:S(2)}) collective-permute-start(bf16[96,512]{1,0:T(8,128)(2,1)S(1)} %get-tuple-element.48), channel_id=1, source_target_pairs={{0,1},{1,0},{2,3},{3,2},{4,5},{5,4},{6,7},{7,6},{8,9},{9,8},{10,11... | collective-permute-start | bytes 294920 | tf_op jit(solution)/shard_map/ppermute | solution.py:370
  38.2 10.3 %collective-permute-start.12 = (bf16[96,512]{1,0:T(8,128)(2,1)S(1)}, bf16[96,512]{1,0:T(8,128)(2,1)S(1)}, u32[]{:S(2)}, u32[]{:S(2)}) collective-permute-start(bf16[96,512]{1,0:T(8,128)(2,1)S(1)} %get-tuple-element.49), channel_id=1, source_target_pairs={{0,4},{1,5},{2,6},{3,7},{4,0},{5,1},{6,2},{7,3},{8,12},{9,13},{10,... | collective-permute-start | bytes 294920 | tf_op jit(solution)/shard_map/ppermute | solution.py:370
  39.3 10.2 %collective-permute-start.13 = (bf16[96,512]{1,0:T(8,128)(2,1)S(1)}, bf16[96,512]{1,0:T(8,128)(2,1)S(1)}, u32[]{:S(2)}, u32[]{:S(2)}) collective-permute-start(bf16[96,512]{1,0:T(8,128)(2,1)S(1)} %get-tuple-element.50), channel_id=1, source_target_pairs={{0,5},{1,4},{2,7},{3,6},{4,1},{5,0},{6,3},{7,2},{8,13},{9,12},{10,... | collective-permute-start | bytes 294920 | tf_op jit(solution)/shard_map/ppermute | solution.py:370
  47.6 13.9 %copy-start.2 = (s32[160,256]{1,0:T(8,128)S(1)}, s32[160,256]{1,0:T(8,128)}, u32[]{:S(2)}) copy-start(s32[160,256]{1,0:T(8,128)} %refs_0_.1) | copy-start | bytes 491524
  50.2 7.1 %collective-permute-start.14 = (bf16[160,512]{1,0:T(8,128)(2,1)S(1)}, bf16[160,512]{1,0:T(8,128)(2,1)S(1)}, u32[]{:S(2)}, u32[]{:S(2)}) collective-permute-start(bf16[160,512]{1,0:T(8,128)(2,1)S(1)} %get-tuple-element.52), channel_id=1, source_target_pairs={{0,8},{8,0},{16,24},{24,16},{1,9},{9,1},{17,25},{25,17},{2,10},{10... | collective-permute-start | bytes 491528 | tf_op jit(solution)/shard_map/ppermute | solution.py:370
  51.7 9.7 %collective-permute-start.15 = (bf16[160,512]{1,0:T(8,128)(2,1)S(1)}, bf16[160,512]{1,0:T(8,128)(2,1)S(1)}, u32[]{:S(2)}, u32[]{:S(2)}) collective-permute-start(bf16[160,512]{1,0:T(8,128)(2,1)S(1)} %get-tuple-element.53), channel_id=1, source_target_pairs={{0,16},{8,24},{16,0},{24,8},{1,17},{9,25},{17,1},{25,9},{2,18},{10... | collective-permute-start | bytes 491528 | tf_op jit(solution)/shard_map/ppermute | solution.py:370
  53.2 8.2 %collective-permute-start.16 = (bf16[160,512]{1,0:T(8,128)(2,1)S(1)}, bf16[160,512]{1,0:T(8,128)(2,1)S(1)}, u32[]{:S(2)}, u32[]{:S(2)}) collective-permute-start(bf16[160,512]{1,0:T(8,128)(2,1)S(1)} %get-tuple-element.54), channel_id=1, source_target_pairs={{0,24},{8,16},{16,8},{24,0},{1,25},{9,17},{17,9},{25,1},{2,26},{10... | collective-permute-start | bytes 491528 | tf_op jit(solution)/shard_map/ppermute | solution.py:370
